TPU v7x, 512 devices: a whole 4x8x8 slice. The times are simulated.
512 devices in a mesh: graph: 64 (over x, z, core), basis: 8 (over y).
Axes of the slice: x: 4, y: 8, z: 8, core: 2. Of those that a mesh axis runs over, the one named last changes fastest.
Arguments:
- edge_feats: bfloat16 [65536, 512], P(('graph', 'basis')), may hold values from -6 to 6
- pre_weight: bfloat16 [512, 512], replicated, may hold values from -0.25 to 0.25
- down_weight: bfloat16 [512, 64], replicated, may hold values from -0.25 to 0.25
- angle_tiles: bfloat16 [1536, 8, 128, 128], P('graph', 'basis'), may hold values from -0.5 to 0.5
- part_source: int32 [1536], P('graph'), may hold values from 0 to 7
- part_owner: int32 [1536, 1], P('graph'), may hold values from 0 to 63; in each aligned block of 24 rows (0 to 23, 24 to 47, ...) at most 2 rows name the same one
- part_target: int32 [1536], P('graph'), may hold values from 0 to 7
- up_weight: bfloat16 [8, 64, 512], P('basis'), may hold values from -0.25 to 0.25
- res_first: bfloat16 [512, 512], replicated, may hold values from -0.25 to 0.25
- res_second: bfloat16 [512, 512], replicated, may hold values from -0.25 to 0.25
- edge_slot: int32 [512, 128], P(('graph', 'basis')), may hold values from 0 to 31, never falling along the last dimension, each value on 1 to 8 neighbouring positions
- slot_owner: int32 [512, 32, 1], P(('graph', 'basis')), may hold values from 0 to 63; in each aligned block of 32 rows (0 to 31, 32 to 63, ..., all dimensions but the last counted through in order) at most 2 rows name the same one
- slot_atom: int32 [512, 32], P(('graph', 'basis')), may hold values from 0 to 31
- atom_feats: bfloat16 [16384, 512], P(('graph', 'basis')), may hold values from -6 to 6
- atom_first: bfloat16 [512, 512], replicated, may hold values from -0.25 to 0.25
- atom_second: bfloat16 [512, 512], replicated, may hold values from -0.25 to 0.25
Outputs:
- edge_update: bfloat16 [65536, 512], P(('graph', 'basis'))
- atom_update: bfloat16 [16384, 512], P(('graph', 'basis'))
Inputs may be any that keep to these rules, and one draw needn't show every extreme that they name: `part_owner`: the 24 parts of one graph shard name each shard at most 2 times, a bound that some block reaches. `slot_owner`: the 32 slots of one device name each graph shard at most 2 times, a bound that some block reaches. `edge_slot`: along a device's 128 rows the slot never falls; every slot holds 1 to 8 rows, one exactly 8.
All inputs are finite; a program needn't handle non-finite values.
Results may differ from a plain program's by a relative error of at most 0.015.
Values may be sent and summed in bfloat16 or wider, within the bound.
No kernel may reach another device: no remote copies, remote signals or barrier semaphores. Data moves between devices by JAX's collectives and lax.ppermute only.
A program may use at most 64 MiB of HBM per device.

v0:
```python
import jax
import jax.numpy as jnp
from jax import lax
from jax.sharding import PartitionSpec as P

half_root = 0.5**0.5


def slot_ranks(target, peer_count, capacity):
    peer_ids = jnp.arange(peer_count, dtype=jnp.int32)
    picked = (target[:, None] == peer_ids[None, :]).astype(jnp.int32)
    earlier = jnp.cumsum(picked, axis=0) - picked
    return target * capacity + jnp.sum(earlier * picked, axis=1)


def slot_owners(positions, slot_total):
    places = jnp.arange(slot_total, dtype=jnp.int32)
    matches = positions[None, :] == places[:, None]
    filled = jnp.any(matches, axis=1)
    item_ids = jnp.arange(positions.shape[0], dtype=jnp.int32)
    owners = jnp.sum(jnp.where(matches, item_ids[None, :], 0), axis=1)
    return (owners, filled)


def body(
    edge_feats,
    pre_weight,
    down_weight,
    angle_tiles,
    part_source,
    part_owner,
    part_target,
    up_weight,
    res_first,
    res_second,
    edge_slot,
    slot_owner,
    slot_atom,
    atom_feats,
    atom_first,
    atom_second,
):
    block_rows = angle_tiles.shape[2]
    narrow = down_weight.shape[1]
    projected = jax.nn.silu(
        jnp.dot(edge_feats, pre_weight, preferred_element_type=jnp.float32)
    ).astype(jnp.bfloat16)
    lowered = jax.nn.silu(
        jnp.dot(projected, down_weight, preferred_element_type=jnp.float32)
    ).astype(jnp.bfloat16)
    shard_rows = lowered.shape[0]
    packed = lowered.reshape(shard_rows * narrow // 128, 128)
    whole_rows = lax.all_gather(packed, "basis", axis=0, tiled=True)
    blocks = whole_rows.reshape(-1, block_rows, narrow)
    count_blocks = blocks.shape[0]
    sources = blocks[part_source]
    products = jnp.einsum(
        "pij,pjk->pik", angle_tiles[:, 0], sources, preferred_element_type=jnp.float32
    ).astype(jnp.bfloat16)
    flat_products = products.reshape(products.shape[0], block_rows * narrow)
    peer_count = lax.axis_size("graph")
    parts_here = part_source.shape[0]
    capacity = max(2, 2 * parts_here // peer_count)
    positions = slot_ranks(part_owner[:, 0], peer_count, capacity)
    owners, filled = slot_owners(positions, peer_count * capacity)
    outgoing = jnp.where(filled[:, None], flat_products[owners], jnp.zeros((), jnp.bfloat16))
    out_target = jnp.where(filled, part_target[owners], -1)
    arrived, arrived_target = (
        lax.all_to_all(outgoing, "graph", split_axis=0, concat_axis=0, tiled=True),
        lax.all_to_all(out_target, "graph", split_axis=0, concat_axis=0, tiled=True),
    )
    block_ids = jnp.arange(count_blocks, dtype=jnp.int32)
    selector = (arrived_target[None, :] == block_ids[:, None]).astype(jnp.bfloat16)
    summed = jnp.dot(selector, arrived, preferred_element_type=jnp.float32)
    paired = summed.reshape(count_blocks * block_rows, narrow).astype(jnp.bfloat16)
    triplet = lax.psum_scatter(
        jnp.dot(paired, up_weight[0], preferred_element_type=jnp.float32).astype(jnp.bfloat16),
        "basis",
        scatter_dimension=0,
        tiled=True,
    ).astype(jnp.float32)
    joined = (edge_feats.astype(jnp.float32) + triplet).astype(jnp.bfloat16)
    inner_act = jax.nn.silu(jnp.dot(joined, res_first, preferred_element_type=jnp.float32)).astype(
        jnp.bfloat16
    )
    second = jax.nn.silu(jnp.dot(inner_act, res_second, preferred_element_type=jnp.float32))
    edge_update = ((joined.astype(jnp.float32) + second) * half_root).astype(jnp.bfloat16)
    slot_count = slot_owner.shape[1]
    slot_ids = jnp.arange(slot_count, dtype=jnp.int32)
    slot_select = (edge_slot[0][None, :] == slot_ids[:, None]).astype(jnp.bfloat16)
    slot_sums = jnp.dot(slot_select, edge_update, preferred_element_type=jnp.float32).astype(
        jnp.bfloat16
    )
    atom_cap = max(2, 2 * slot_count // peer_count)
    atom_places = slot_ranks(slot_owner[0, :, 0], peer_count, atom_cap)
    atom_owners, atom_filled = slot_owners(atom_places, peer_count * atom_cap)
    atom_out = jnp.where(atom_filled[:, None], slot_sums[atom_owners], jnp.zeros((), jnp.bfloat16))
    atom_target = jnp.where(atom_filled, slot_atom[0][atom_owners], -1)
    atom_arrived, atom_arrived_target = (
        lax.all_to_all(atom_out, "graph", split_axis=0, concat_axis=0, tiled=True),
        lax.all_to_all(atom_target, "graph", split_axis=0, concat_axis=0, tiled=True),
    )
    atom_ids = jnp.arange(atom_feats.shape[0], dtype=jnp.int32)
    atom_select = (atom_arrived_target[None, :] == atom_ids[:, None]).astype(jnp.bfloat16)
    gathered = jnp.dot(atom_select, atom_arrived, preferred_element_type=jnp.float32).astype(
        jnp.bfloat16
    )
    hidden = jax.nn.silu(jnp.dot(gathered, atom_first, preferred_element_type=jnp.float32)).astype(
        jnp.bfloat16
    )
    atom_update = (
        atom_feats.astype(jnp.float32)
        + jnp.dot(hidden, atom_second, preferred_element_type=jnp.float32)
    ).astype(jnp.bfloat16)
    return (edge_update, atom_update)


def solution(mesh):
    in_specs = (
        P(("graph", "basis"), None),
        P(),
        P(),
        P("graph", "basis", None, None),
        P("graph"),
        P("graph", None),
        P("graph"),
        P("basis", None, None),
        P(),
        P(),
        P(("graph", "basis"), None),
        P(("graph", "basis"), None, None),
        P(("graph", "basis"), None),
        P(("graph", "basis"), None),
        P(),
        P(),
    )
    out_specs = (P(("graph", "basis"), None), P(("graph", "basis"), None))
    return jax.shard_map(body, mesh=mesh, in_specs=in_specs, out_specs=out_specs, check_vma=False)
```

profile of v0, /device:TPU:1, one launch (start us, length us, event | category | flops | bytes accessed | tf_op | source)
XLA Modules:
  0.0 220.9 jit_solution(17062941200675804355)
XLA Ops:
  7.2 0.0 copy-start
  7.2 0.8 fusion.12
  8.0 0.8 select_reduce_fusion.3
  8.9 0.7 multiply_add_fusion.1
  9.5 0.1 fusion.11
  9.6 0.1 select_reduce_fusion.2
  9.7 2.1 fusion.22
  11.8 1.5 fusion.23
  13.3 15.0 %fusion.17 = s32[128]{0:T(128)S(1)} fusion(pred[128]{0:T(512)(128)(4,1)S(1)} %fusion.11, s32[]{:T(128)} %bitcast.3, s32[]{:T(128)} %bitcast.4, s32[]{:T(128)} %bitcast.5, s32[]{:T(128)} %bitcast.6, s32[]{:T(128)} %bitcast.7, s32[]{:T(128)} %bitcast.8, s32[]{:T(128)} %bitcast.9, s32[]{:T(128)} %bitcast.10, s32[]{:T(128)} %bitcast.11, s32[]{:T(128)} %bitcast.12, ...), kind=kLoop, calls=%fused_computation.74 | loop fusion | flops 6400 | bytes 1248 | tf_op jit(solution)/shard_map/jit(_where)/select_n | solution.py:67
  28.3 0.8 select_n.73
  29.0 14.8 %all-to-all-start = ((s32[64,2,1]{1,2,0:T(1,128)}), s32[64,2,1]{1,2,0:T(1,128)S(1)}, u32[]{:S(2)}, u32[]{:S(2)}) async-start(s32[64,2,1]{1,2,0:T(1,128)} %bitcast.27), calls=%async_computation | async-start | bytes 65536 | tf_op jit(solution)/shard_map/all_to_all | solution.py:70
  43.9 0.1 broadcast_in_dim.82
  44.0 1.5 multiply_convert_fusion.8
  45.5 0.1 copy.27
  45.7 0.1 reshape.122
  45.8 20.7 %all_gather.3 = bf16[512,128]{1,0:T(8,128)(2,1)S(1)} all-gather(bf16[64,128]{1,0:T(8,128)(2,1)S(1)} %reshape.122), channel_id=1, replica_groups=mesh['graph'=64,'basis'=8] {'basis'}, dimensions={0}, use_global_device_ids=true | all-gather | bytes 147456 | tf_op jit(solution)/shard_map/all_gather | solution.py:53
  66.5 0.1 reshape.123
  66.6 0.1 copy.28
  66.8 0.6 gather_fusion
  67.5 0.6 fusion
  68.1 0.4 copy.29
  68.5 0.6 reshape.124
  69.1 3.2 %gather_fusion.1 = bf16[128,8192]{1,0:T(8,128)(2,1)} fusion(bf16[24,8192]{1,0:T(8,128)(2,1)S(1)} %reshape.124, s32[1024]{0:T(1024)S(1)} %pad_clamp_fusion.1), kind=kCustom, calls=%fused_computation.1 | custom fusion | bytes 4194816 | tf_op jit(solution)/shard_map/gather | solution.py:66
  72.4 3.2 %gather.22 = bf16[64,2,8192]{2,1,0:T(2,128)(2,1)S(1)} reshape(bf16[128,8192]{1,0:T(8,128)(2,1)} %gather_fusion.1) | data formatting | bytes 4194304 | tf_op jit(solution)/shard_map/gather | solution.py:66
  75.5 3.2 %broadcast_select_fusion = bf16[64,2,8192]{2,1,0:T(2,128)(2,1)} fusion(bf16[64,2,8192]{2,1,0:T(2,128)(2,1)S(1)} %gather.22, pred[64,2]{1,0:T(8,128)(4,1)S(1)} %broadcast_in_dim.82), kind=kLoop, calls=%fused_computation.5 | loop fusion | flops 1048576 | bytes 4194432 | tf_op jit(solution)/shard_map/jit(_where)/select_n | solution.py:66
  78.7 15.8 %all-to-all-start.1 = ((bf16[64,2,8192]{2,1,0:T(2,128)(2,1)}), bf16[64,2,8192]{2,1,0:T(2,128)(2,1)S(1)}, u32[]{:S(2)}, u32[]{:S(2)}) async-start(bf16[64,2,8192]{2,1,0:T(2,128)(2,1)} %broadcast_select_fusion), calls=%async_computation.1 | async-start | bytes 4194304 | tf_op jit(solution)/shard_map/all_to_all | solution.py:69
  94.5 0.0 reduce-scatter.2.cloned.1.call-start
  94.6 0.5 broadcast.228
  95.1 0.7 reduce.6
  95.8 0.1 eq.103
  96.0 49.8 %all-to-all-done.1 = bf16[64,2,8192]{2,1,0:T(2,128)(2,1)S(1)} async-done(((bf16[64,2,8192]{2,1,0:T(2,128)(2,1)}), bf16[64,2,8192]{2,1,0:T(2,128)(2,1)S(1)}, u32[]{:S(2)}, u32[]{:S(2)}) %all-to-all-start.1) | async-done | bytes 2097184 | tf_op jit(solution)/shard_map/all_to_all | solution.py:69
  145.7 2.2 %all_to_all.22 = bf16[128,8192]{1,0:T(8,128)(2,1)} reshape(bf16[64,2,8192]{2,1,0:T(2,128)(2,1)S(1)} %all-to-all-done.1) | data formatting | bytes 4194304 | tf_op jit(solution)/shard_map/all_to_all | solution.py:69
  148.0 2.0 convolution_convert_fusion
  150.0 0.0 copy-start.11
  150.0 0.2 convert_element_type.70
  150.2 1.4 convolution_convert_fusion.1
  151.6 0.0 reduce-scatter.2.cloned.1.call-update
  151.7 0.1 fusion.10
  151.8 0.1 reduce_window_sum.23
  151.8 0.2 select_reduce_fusion.1
  152.0 0.1 select_reduce_fusion
  152.1 0.0 copy-start.8
  152.1 1.2 gather_fusion.2
  153.4 0.1 fusion.9
  153.5 0.8 select_n.79
  154.2 5.8 %all-to-all-start.2 = ((s32[64,2,1]{1,2,0:T(1,128)}), s32[64,2,1]{1,2,0:T(1,128)S(1)}, u32[]{:S(2)}, u32[]{:S(2)}) async-start(s32[64,2,1]{1,2,0:T(1,128)} %bitcast.35), calls=%async_computation.3 | async-start | bytes 65536 | tf_op jit(solution)/shard_map/all_to_all | solution.py:101
  160.1 0.1 broadcast_in_dim.88
  160.2 23.6 %reduce-scatter.2.cloned.1.call-done = bf16[128,512]{1,0:T(8,128)(2,1)} async-done(((bf16[1024,512]{1,0:T(8,128)(2,1)}), bf16[128,512]{1,0:T(8,128)(2,1)}) %reduce-scatter.2.cloned.1.call-update) | async-done | bytes 131088 | tf_op jit(solution)/shard_map/reduce_scatter | solution.py:76
  183.9 1.5 multiply_convert_fusion
  185.4 0.0 copy-start.4
  185.4 0.0 copy-start.3
  185.4 0.0 copy-start.2
  185.4 0.0 copy-start.6
  185.4 0.1 convolution_convert_fusion.4
  185.5 0.9 gather_fusion.3
  186.4 0.1 gather.25
  186.5 0.8 broadcast_select_fusion.1
  187.3 15.2 %all-to-all-start.3 = ((bf16[64,2,512]{2,1,0:T(2,128)(2,1)}), bf16[64,2,512]{2,1,0:T(2,128)(2,1)S(1)}, u32[]{:S(2)}, u32[]{:S(2)}) async-start(bf16[64,2,512]{2,1,0:T(2,128)(2,1)} %broadcast_select_fusion.1), calls=%async_computation.4 | async-start | bytes 262144 | tf_op jit(solution)/shard_map/all_to_all | solution.py:100
  202.5 0.7 reduce.7
  203.2 0.1 eq.113
  203.3 9.5 %all-to-all-done.3 = bf16[64,2,512]{2,1,0:T(2,128)(2,1)S(1)} async-done(((bf16[64,2,512]{2,1,0:T(2,128)(2,1)}), bf16[64,2,512]{2,1,0:T(2,128)(2,1)S(1)}, u32[]{:S(2)}, u32[]{:S(2)}) %all-to-all-start.3) | async-done | bytes 131104 | tf_op jit(solution)/shard_map/all_to_all | solution.py:100
  212.8 0.1 all_to_all.25
  212.9 0.3 multiply_convert_fusion.7
  213.2 0.8 fusion.1
  (30 shorter events, 0.1 us)
Async XLA Ops:
  7.2 60.3 %copy-start = (bf16[24,1,128,128]{3,2,1,0:T(8,128)(2,1)S(1)}, bf16[24,1,128,128]{3,2,1,0:T(8,128)(2,1)}, u32[]{:S(2)}) copy-start(bf16[24,1,128,128]{3,2,1,0:T(8,128)(2,1)} %param.19) | copy-start | bytes 2359300
  7.2 59.6 %copy-start.12 = (s32[24]{0:T(128)S(1)}, s32[24]{0:T(128)}, u32[]{:S(2)}) copy-start(s32[24]{0:T(128)} %param.20) | copy-start | bytes 292
  29.0 49.7 %all-to-all-start = ((s32[64,2,1]{1,2,0:T(1,128)}), s32[64,2,1]{1,2,0:T(1,128)S(1)}, u32[]{:S(2)}, u32[]{:S(2)}) async-start(s32[64,2,1]{1,2,0:T(1,128)} %bitcast.27), calls=%async_computation | async-start | bytes 65536 | tf_op jit(solution)/shard_map/all_to_all | solution.py:70
  78.7 67.0 %all-to-all-start.1 = ((bf16[64,2,8192]{2,1,0:T(2,128)(2,1)}), bf16[64,2,8192]{2,1,0:T(2,128)(2,1)S(1)}, u32[]{:S(2)}, u32[]{:S(2)}) async-start(bf16[64,2,8192]{2,1,0:T(2,128)(2,1)} %broadcast_select_fusion), calls=%async_computation.1 | async-start | bytes 4194304 | tf_op jit(solution)/shard_map/all_to_all | solution.py:69
  94.5 89.3 %reduce-scatter.2.cloned.1.call-start = ((), (), s32[]{:S(2)}) async-start(), calls=%async_computation.5 | async-start | bytes 1179648 | tf_op jit(solution)/shard_map/reduce_scatter | solution.py:76
  148.0 2.3 %copy-start.5 = (bf16[1,64,512]{2,1,0:T(8,128)(2,1)S(1)}, bf16[1,64,512]{2,1,0:T(8,128)(2,1)}, u32[]{:S(2)}) copy-start(bf16[1,64,512]{2,1,0:T(8,128)(2,1)} %param.23) | copy-start | bytes 196612
  148.0 3.7 %copy-start.7 = (s32[1,32,1]{1,2,0:T(1,128)S(1)}, s32[1,32,1]{1,2,0:T(1,128)}, u32[]{:S(2)}) copy-start(s32[1,32,1]{1,2,0:T(1,128)} %param.27) | copy-start | bytes 388
  148.0 4.2 %copy-start.1 = (s32[1,32]{1,0:T(1,128)S(1)}, s32[1,32]{1,0:T(1,128)}, u32[]{:S(2)}) copy-start(s32[1,32]{1,0:T(1,128)} %param.28) | copy-start | bytes 388
  150.0 33.9 %copy-start.9 = (bf16[512,512]{1,0:T(8,128)(2,1)S(1)}, bf16[512,512]{1,0:T(8,128)(2,1)}, u32[]{:S(2)}) copy-start(bf16[512,512]{1,0:T(8,128)(2,1)} %param.25) | copy-start | bytes 1572868
  150.0 33.9 %copy-start.10 = (bf16[512,512]{1,0:T(8,128)(2,1)S(1)}, bf16[512,512]{1,0:T(8,128)(2,1)}, u32[]{:S(2)}) copy-start(bf16[512,512]{1,0:T(8,128)(2,1)} %param.24) | copy-start | bytes 1572868
  150.0 33.9 %copy-start.11 = (bf16[128,512]{1,0:T(8,128)(2,1)S(1)}, bf16[128,512]{1,0:T(8,128)(2,1)}, u32[]{:S(2)}) copy-start(bf16[128,512]{1,0:T(8,128)(2,1)} %param.16) | copy-start | bytes 393220
  152.1 33.3 %copy-start.8 = (s32[1,128]{1,0:T(1,128)S(1)}, s32[1,128]{1,0:T(1,128)}, u32[]{:S(2)}) copy-start(s32[1,128]{1,0:T(1,128)} %param.26) | copy-start | bytes 1540
  154.2 33.1 %all-to-all-start.2 = ((s32[64,2,1]{1,2,0:T(1,128)}), s32[64,2,1]{1,2,0:T(1,128)S(1)}, u32[]{:S(2)}, u32[]{:S(2)}) async-start(s32[64,2,1]{1,2,0:T(1,128)} %bitcast.35), calls=%async_computation.3 | async-start | bytes 65536 | tf_op jit(solution)/shard_map/all_to_all | solution.py:101
  185.4 28.7 %copy-start.4 = (bf16[128,512]{1,0:T(8,128)(2,1)}, bf16[128,512]{1,0:T(8,128)(2,1)S(1)}, u32[]{:S(2)}) copy-start(bf16[128,512]{1,0:T(8,128)(2,1)S(1)} %multiply_convert_fusion) | copy-start | bytes 393220
  185.4 27.5 %copy-start.3 = (bf16[512,512]{1,0:T(8,128)(2,1)S(1)}, bf16[512,512]{1,0:T(8,128)(2,1)}, u32[]{:S(2)}) copy-start(bf16[512,512]{1,0:T(8,128)(2,1)} %param.30) | copy-start | bytes 1572868
  185.4 27.8 %copy-start.2 = (bf16[512,512]{1,0:T(8,128)(2,1)S(1)}, bf16[512,512]{1,0:T(8,128)(2,1)}, u32[]{:S(2)}) copy-start(bf16[512,512]{1,0:T(8,128)(2,1)} %param.31) | copy-start | bytes 1572868
  185.4 27.8 %copy-start.6 = (bf16[32,512]{1,0:T(8,128)(2,1)S(1)}, bf16[32,512]{1,0:T(8,128)(2,1)}, u32[]{:S(2)}) copy-start(bf16[32,512]{1,0:T(8,128)(2,1)} %param.29) | copy-start | bytes 98308
  187.3 25.5 %all-to-all-start.3 = ((bf16[64,2,512]{2,1,0:T(2,128)(2,1)}), bf16[64,2,512]{2,1,0:T(2,128)(2,1)S(1)}, u32[]{:S(2)}, u32[]{:S(2)}) async-start(bf16[64,2,512]{2,1,0:T(2,128)(2,1)} %broadcast_select_fusion.1), calls=%async_computation.4 | async-start | bytes 262144 | tf_op jit(solution)/shard_map/all_to_all | solution.py:100
Sparse Core Ops, SparseCore 0:
  151.8 32.0 reduce-scatter.1
where the time goes:
time: 222 us; the launch traced here: 221 us
  waiting for transfers between devices  83 us (37%)
  starting transfers between devices  51.7 us (23%)
  other arithmetic  23.4 us (11%)
  blocking collectives  20.7 us (9%)
  local copies, waits for them, and re-layouts  19.4 us (9%)
  between operations  14.4 us (6%)
  matrix products  8.27 us (4%)
    all_to_all x1, waiting for transfers between devices, body(): lax.all_to_all(outgoing, 'graph', split_axis=0, concat_axis=0, tiled=True)  49.8 us
    reduce_scatter x1, waiting for transfers between devices, body(): lax.psum_scatter(jnp.dot(paired, up_weight[0], preferred_element_type=jnp...  23.6 us
    all_gather x1, blocking collectives, body(): whole_rows = lax.all_gather(packed, 'basis', axis=0, tiled=True)  20.7 us
    all_to_all x1, starting transfers between devices, body(): lax.all_to_all(outgoing, 'graph', split_axis=0, concat_axis=0, tiled=True)  15.8 us
    all_to_all x1, starting transfers between devices, body(): lax.all_to_all(atom_out, 'graph', split_axis=0, concat_axis=0, tiled=True)  15.2 us
    select_n x2, other arithmetic, body(): out_target = jnp.where(filled, part_target[owners], -1)  15 us
    all_to_all x1, starting transfers between devices, body(): lax.all_to_all(out_target, 'graph', split_axis=0, concat_axis=0, tiled=True)  14.8 us
    all_to_all x1, waiting for transfers between devices, body(): lax.all_to_all(atom_out, 'graph', split_axis=0, concat_axis=0, tiled=True)  9.49 us
  transfers between devices with their start and end apart: 5, of which 3 were waited for; matrix products, arithmetic and copies ran while one was open for 10% of the time, Pallas kernels for 0%

commit v1 on v0

v1 whole, which is shorter than its diff:
```python
import jax
import jax.numpy as jnp
from jax import lax
from jax.experimental import pallas as pl
from jax.experimental.pallas import tpu as pltpu
from jax.sharding import PartitionSpec as P

half_root = 0.5**0.5
f32, bf16, i32 = jnp.float32, jnp.bfloat16, jnp.int32
VMEM = pl.BlockSpec(memory_space=pltpu.VMEM)
SMEM = pl.BlockSpec(memory_space=pltpu.SMEM)
HEAD = 8


def iota(shape, axis):
    return lax.broadcasted_iota(i32, shape, axis)


def silu(v):
    return v / (1.0 + jnp.exp(-v))


def dot(a, b, left, right):
    return lax.dot_general(a, b, (((left,), (right,)), ((), ())), preferred_element_type=f32)


def lower_kernel(edge_ref, pre_ref, down_ref, out_ref):
    projected = silu(dot(edge_ref[...], pre_ref[...], 1, 0)).astype(bf16)
    lowered = silu(dot(down_ref[...], projected, 1, 1)).astype(bf16)
    for i in range(out_ref.shape[0]):
        out_ref[i] = lowered


def column(row):
    n = row.shape[1]
    return jnp.sum(jnp.where(iota((n, n), 0) == iota((n, n), 1), row, 0), axis=1, keepdims=True)


def table_kernel(me_ref, owner_ref, target_ref, slot_ref, slot_owner_ref, slot_atom_ref, head_ref, atoms_ref):
    me = me_ref[0]
    parts = owner_ref.shape[1]
    base = (me % 4) * 32
    slots = slot_owner_ref.shape[1]
    rows = slot_ref.shape[1]
    place = iota((parts, 128), 1) == iota((parts, 128), 0) + base
    owner_row = jnp.sum(jnp.where(place, column(owner_ref[...]), 0), axis=0, keepdims=True)
    target_row = jnp.sum(jnp.where(place, column(target_ref[...]), 0), axis=0, keepdims=True)
    own_row = slot_owner_ref[...]
    own_col = column(own_row)
    same = own_col == own_row
    down, right = iota((slots, slots), 0), iota((slots, slots), 1)
    rank_row = jnp.sum(jnp.where(same & (down < right), 1, 0), axis=0, keepdims=True)
    rank_col = jnp.sum(jnp.where(same & (right < down), 1, 0), axis=1, keepdims=True)
    spot_col = own_col * 2 + rank_col
    spot_row = jnp.sum(
        jnp.where(slot_ref[...] == iota((slots, rows), 0), spot_col, 0), axis=0, keepdims=True
    )
    sub = iota((HEAD, 128), 0)
    head = jnp.where(sub == 0, owner_row, jnp.where(sub == 1, target_row, jnp.where(sub == 2, spot_row, 0)))
    head_ref[...] = head.astype(f32)
    peers = atoms_ref.shape[0]
    atom = slot_atom_ref[...] + 1
    mine = iota((peers, slots), 0) == own_row
    first = jnp.sum(jnp.where(mine & (rank_row == 0), atom, 0), axis=1, keepdims=True)
    second = jnp.sum(jnp.where(mine & (rank_row == 1), atom, 0), axis=1, keepdims=True)
    lane = iota((peers, 128), 1)
    atoms = jnp.where(lane == 2 * me, first, jnp.where(lane == 2 * me + 1, second, 0))
    atoms_ref[...] = atoms.astype(f32)


def product_kernel(source_ref, lowered_ref, tiles_ref, head_ref, atoms_ref, out_ref, scratch):
    parts = tiles_ref.shape[0]
    peers, rows, _ = out_ref.shape
    for p in range(parts):
        product = dot(lowered_ref[source_ref[p]], tiles_ref[p], 1, 1)
        scratch[pl.ds(p, peers, stride=rows), :] = product
    scratch[pl.ds(parts, peers, stride=rows), :] = jnp.broadcast_to(head_ref[0:1, :], (peers, 128))
    scratch[pl.ds(parts + 1, peers, stride=rows), :] = jnp.broadcast_to(head_ref[1:2, :], (peers, 128))
    scratch[pl.ds(parts + 2, peers, stride=rows), :] = atoms_ref[...]
    for r in range(parts + 3, rows):
        scratch[pl.ds(r, peers, stride=rows), :] = jnp.zeros((peers, 128), f32)
    for k in range(peers):
        out_ref[k] = scratch[pl.ds(k * rows, rows), :].astype(bf16)


def combine_kernel(parts, blocks, arrived_ref, out_ref, atoms_ref):
    peers, rows, _ = arrived_ref.shape
    group = 128 // rows
    targets = peers * blocks
    head = arrived_ref[:, parts:rows, :].astype(f32)
    head = jnp.sum(head.reshape(peers // group, group, rows - parts, 128), axis=1)
    atoms_ref[...] = jnp.sum(head, axis=0)
    lane = iota((1, 128), 1)
    valid = (lane % rows) < parts
    row = iota((targets, 128), 0).astype(f32)
    total = jnp.zeros((targets, 128), f32)
    for r in range(0, peers // group, 2):
        hits = []
        for q in (r, r + 1):
            ids = head[q, 1:2, :] * float(peers) + head[q, 0:1, :]
            ids = jnp.where(valid, ids, -1.0)
            hits.append(jnp.where(row == ids, 1.0, 0.0).astype(bf16))
        items = arrived_ref[r * group : (r + 2) * group].reshape(2 * 128, 128)
        total = total + dot(jnp.concatenate(hits, axis=1), items, 1, 0)
    out_ref[...] = total


def edge_kernel(columns_ref, up_ref, edge_ref, first_ref, second_ref, head_ref, out_ref, send_ref, scratch):
    triplet = dot(columns_ref[...].astype(bf16), up_ref[...], 0, 0)
    joined = (edge_ref[...].astype(f32) + triplet).astype(bf16)
    inner = silu(dot(joined, first_ref[...], 1, 0)).astype(bf16)
    second = silu(dot(inner, second_ref[...], 1, 0))
    update = ((joined.astype(f32) + second) * half_root).astype(bf16)
    out_ref[...] = update
    places = send_ref.shape[0] * 2
    chunks = update.shape[1] // 128
    spot = iota((places, update.shape[0]), 0).astype(f32) == head_ref[2:3, :]
    sums = dot(jnp.where(spot, 1.0, 0.0).astype(bf16), update, 1, 0)
    for c in range(chunks):
        scratch[pl.ds(c, places, stride=chunks), :] = sums[:, c * 128 : (c + 1) * 128]
    send_ref[...] = scratch[...].reshape(send_ref.shape).astype(bf16)


def atom_kernel(arrived_ref, ids_ref, feats_ref, first_ref, second_ref, out_ref, scratch):
    places = arrived_ref.shape[0] * 2
    count, width = feats_ref.shape
    chunks = width // 128
    scratch[...] = arrived_ref[...].astype(f32).reshape(scratch.shape)
    hit = (iota((count, places), 0) + 1).astype(f32) == ids_ref[2:3, :]
    hit = jnp.where(hit, 1.0, 0.0).astype(bf16)
    gathered = jnp.concatenate(
        [
            dot(hit, scratch[pl.ds(c, places, stride=chunks), :].astype(bf16), 1, 0)
            for c in range(chunks)
        ],
        axis=1,
    ).astype(bf16)
    hidden = silu(dot(gathered, first_ref[...], 1, 0)).astype(bf16)
    out_ref[...] = (feats_ref[...].astype(f32) + dot(hidden, second_ref[...], 1, 0)).astype(bf16)


def call(kernel, name, specs, outs, *args, scratch=()):
    return pl.pallas_call(
        kernel,
        name=name,
        in_specs=specs,
        out_specs=[VMEM] * len(outs),
        out_shape=[jax.ShapeDtypeStruct(shape, dtype) for shape, dtype in outs],
        scratch_shapes=scratch,
    )(*args)


def body(
    edge_feats,
    pre_weight,
    down_weight,
    angle_tiles,
    part_source,
    part_owner,
    part_target,
    up_weight,
    res_first,
    res_second,
    edge_slot,
    slot_owner,
    slot_atom,
    atom_feats,
    atom_first,
    atom_second,
):
    peers, blocks = lax.axis_size("graph"), lax.axis_size("basis")
    parts = part_source.shape[0]
    narrow = down_weight.shape[1]
    rows, width = edge_feats.shape
    packed = -(-(parts + 3) // 8) * 8
    me = lax.axis_index("graph").astype(i32).reshape(1)

    (lowered,) = call(
        lower_kernel, "lower", [VMEM] * 3, [((blocks, narrow, rows), bf16)],
        edge_feats, pre_weight, down_weight.T,
    )
    lowered = lax.all_to_all(lowered, "basis", 0, 0, tiled=True)
    head, atoms = call(
        table_kernel, "tables", [SMEM] + [VMEM] * 5,
        [((HEAD, 128), f32), ((peers, 128), f32)],
        me, part_owner.reshape(1, parts), part_target.reshape(1, parts), edge_slot,
        slot_owner.reshape(1, -1), slot_atom,
    )
    (send,) = call(
        product_kernel, "products", [SMEM] + [VMEM] * 4, [((peers, packed, 128), bf16)],
        part_source, lowered, angle_tiles.reshape(parts, rows, rows), head, atoms,
        scratch=[pltpu.VMEM((peers * packed, 128), f32)],
    )
    arrived = lax.all_to_all(send, "graph", 0, 0, tiled=True)
    ups = jnp.broadcast_to(up_weight, (blocks, narrow, width))
    ups, _ = lax.optimization_barrier((ups, send))
    ups = lax.all_to_all(ups, "basis", 0, 0, tiled=True)
    summed, ids = call(
        lambda *refs: combine_kernel(parts, blocks, *refs), "combine", [VMEM],
        [((peers * blocks, 128), f32), ((packed - parts, 128), f32)],
        arrived,
    )
    columns = lax.all_to_all(
        summed.reshape(peers * blocks, 1, 128), ("basis", "graph"), 0, 0, tiled=True
    )
    edge_update, send = call(
        edge_kernel, "edges", [VMEM] * 6,
        [((rows, width), bf16), ((peers, 2 * width // 128, 128), bf16)],
        columns.reshape(peers * blocks, 128), ups.reshape(blocks * narrow, width), edge_feats,
        res_first, res_second, head,
        scratch=[pltpu.VMEM((peers * 2 * width // 128, 128), f32)],
    )
    arrived = lax.all_to_all(send, "graph", 0, 0, tiled=True)
    (atom_update,) = call(
        atom_kernel, "atoms", [VMEM] * 5, [(atom_feats.shape, bf16)],
        arrived, ids, atom_feats, atom_first, atom_second,
        scratch=[pltpu.VMEM((peers * 2 * width // 128, 128), f32)],
    )
    return (edge_update, atom_update)


def solution(mesh):
    in_specs = (
        P(("graph", "basis"), None),
        P(),
        P(),
        P("graph", "basis", None, None),
        P("graph"),
        P("graph", None),
        P("graph"),
        P("basis", None, None),
        P(),
        P(),
        P(("graph", "basis"), None),
        P(("graph", "basis"), None, None),
        P(("graph", "basis"), None),
        P(("graph", "basis"), None),
        P(),
        P(),
    )
    out_specs = (P(("graph", "basis"), None), P(("graph", "basis"), None))
    return jax.shard_map(body, mesh=mesh, in_specs=in_specs, out_specs=out_specs, check_vma=False)
```

time: 222 us -> 127 us (0.57)
  waiting for transfers between devices: 83 us -> 38.4 us
  starting transfers between devices: 51.7 us -> 26.6 us
  blocking collectives: 20.7 us -> 44.3 us
  other arithmetic: 23.4 us -> 0 us
  local copies, waits for them, and re-layouts: 19.4 us -> 1.51 us
  Pallas kernels: 0 us -> 14.6 us
  between operations: 14.4 us -> 0.67 us
  matrix products: 8.27 us -> 0 us
    all_to_all x0 -> x2, blocking collectives: none -> 44.3 us  [the longest x1 28.5 us: body(): lax.all_to_all(summed.reshape(peers * blocks, 1, 128), ('basis', 'graph')...]
    all_to_all x4 -> x3, starting transfers between devices: 51.6 us -> 26.6 us  [the longest x1 15.5 us: body(): arrived = lax.all_to_all(send, 'graph', 0, 0, tiled=True)]
    reduce_scatter x1 -> x0, waiting for transfers between devices: 23.6 us -> none  [body(): lax.psum_scatter(jnp.dot(paired, up_weight[0], preferred_element_type=jnp...]
    all_to_all x4 -> x3, waiting for transfers between devices: 59.3 us -> 38.4 us  [the longest x1 16.4 us: body(): arrived = lax.all_to_all(send, 'graph', 0, 0, tiled=True)]
    all_gather x1 -> x0, blocking collectives: 20.7 us -> none  [body(): whole_rows = lax.all_gather(packed, 'basis', axis=0, tiled=True)]
    select_n x7 -> x0, other arithmetic: 19 us -> none  [the longest x2 15 us: body(): out_target = jnp.where(filled, part_target[owners], -1)]
    pallas_call x0 -> x6, Pallas kernels: none -> 14.6 us  [call(): pl.pallas_call(kernel, name=name, in_specs=specs, out_specs=[VMEM] * len(...]
    gather x8 -> x0, local copies, waits for them, and re-layouts: 12.7 us -> none  [the longest x2 6.38 us: body(): flat_products[owners]]
  transfers between devices with their start and end apart: 5 -> 3, of which waited for: 3 -> 3; matrix products, arithmetic and copies ran while one was open for 10% -> 1% of each run, Pallas kernels for 0% -> 3%
where the time goes in v1:
time: 127 us; the launch traced here: 126 us
  blocking collectives  44.3 us (35%)
  waiting for transfers between devices  38.4 us (30%)
  starting transfers between devices  26.6 us (21%)
  Pallas kernels  14.6 us (11%)
  local copies, waits for them, and re-layouts  1.51 us (1%)
    all_to_all x1, blocking collectives, body(): lax.all_to_all(summed.reshape(peers * blocks, 1, 128), ('basis', 'graph')...  28.5 us
    all_to_all x1, waiting for transfers between devices, body(): arrived = lax.all_to_all(send, 'graph', 0, 0, tiled=True)  16.4 us
    all_to_all x1, blocking collectives, body(): arrived = lax.all_to_all(send, 'graph', 0, 0, tiled=True)  15.8 us
    all_to_all x1, starting transfers between devices, body(): arrived = lax.all_to_all(send, 'graph', 0, 0, tiled=True)  15.5 us
    all_to_all x1, waiting for transfers between devices, body(): ups = lax.all_to_all(ups, 'basis', 0, 0, tiled=True)  15.5 us
    pallas_call x6, Pallas kernels, call(): pl.pallas_call(kernel, name=name, in_specs=specs, out_specs=[VMEM] * len(...  14.6 us
    all_to_all x1, starting transfers between devices, body(): lowered = lax.all_to_all(lowered, 'basis', 0, 0, tiled=True)  7.64 us
    all_to_all x1, waiting for transfers between devices, body(): lowered = lax.all_to_all(lowered, 'basis', 0, 0, tiled=True)  6.48 us
  transfers between devices with their start and end apart: 3, of which 3 were waited for; matrix products, arithmetic and copies ran while one was open for 1% of the time, Pallas kernels for 3%

profile of v1, /device:TPU:1, one launch (start us, length us, event | category | flops | bytes accessed | tf_op | source)
XLA Modules:
  0.0 126.1 jit_solution(2836561275319364051)
XLA Ops:
  0.6 2.2 %lower.1 = bf16[8,64,128]{2,1,0:T(8,128)(2,1)} custom-call(bf16[128,512]{1,0:T(8,128)(2,1)} %edge_ref.3, bf16[512,512]{1,0:T(8,128)(2,1)} %pre_ref.1, bf16[64,512]{1,0:T(8,128)(2,1)} %bitcast.17), custom_call_target="tpu_custom_call" | custom-call | tf_op jit(solution)/shard_map/lower/pallas_call | solution.py:143
  2.8 7.6 %all-to-all-start = ((bf16[8,64,128]{2,1,0:T(8,128)(2,1)}), bf16[8,64,128]{2,1,0:T(8,128)(2,1)S(1)}, u32[]{:S(2)}, u32[]{:S(2)}) async-start(bf16[8,64,128]{2,1,0:T(8,128)(2,1)} %lower.1), calls=%async_computation | async-start | bytes 262144 | tf_op jit(solution)/shard_map/all_to_all | solution.py:182
  10.4 1.5 %tables.1 = (f32[8,128]{1,0:T(8,128)}, f32[64,128]{1,0:T(8,128)}) custom-call(s32[1]{0:T(128)} %bitcast.2.me_ref, s32[1,24]{1,0:T(1,128)} %bitcast.18, s32[1,24]{1,0:T(1,128)} %bitcast.19, s32[1,128]{1,0:T(1,128)} %slot_ref.1, s32[1,32]{1,0:T(1,128)} %bitcast.20, s32[1,32]{1,0:T(1,128)} %slot_atom_ref.1), custom_call_target="tpu_custom_call" | custom-call | tf_op jit(solution)/shard_map/tables/pallas_call | solution.py:143
  12.0 6.5 %all-to-all-done.lowered_ref = bf16[8,64,128]{2,1,0:T(8,128)(2,1)S(1)} async-done(((bf16[8,64,128]{2,1,0:T(8,128)(2,1)}), bf16[8,64,128]{2,1,0:T(8,128)(2,1)S(1)}, u32[]{:S(2)}, u32[]{:S(2)}) %all-to-all-start) | async-done | bytes 131104 | tf_op jit(solution)/shard_map/all_to_all | solution.py:182
  18.5 0.0 copy-start.2
  18.5 0.7 copy-done.2
  19.1 3.1 %products.1 = bf16[64,32,128]{2,1,0:T(8,128)(2,1)} custom-call(s32[24]{0:T(128)} %source_ref.1, bf16[8,64,128]{2,1,0:T(8,128)(2,1)} %copy-done.2, bf16[24,128,128]{2,1,0:T(8,128)(2,1)} %bitcast.14, f32[8,128]{1,0:T(8,128)} %get-tuple-element.9.head_ref, f32[64,128]{1,0:T(8,128)} %get-tuple-element.10.atoms_ref), custom_call_target="tpu_custom_call" | custom-call | tf_op jit(solution)/shard_map/products/pallas_call | solution.py:143
  22.2 0.0 copy-start.3
  22.2 15.5 %all-to-all-start.1 = ((bf16[64,32,128]{2,1,0:T(8,128)(2,1)}), bf16[64,32,128]{2,1,0:T(8,128)(2,1)S(1)}, u32[]{:S(2)}, u32[]{:S(2)}) async-start(bf16[64,32,128]{2,1,0:T(8,128)(2,1)} %products.1), calls=%async_computation.1 | async-start | bytes 1048576 | tf_op jit(solution)/shard_map/all_to_all | solution.py:194
  37.7 0.0 copy-done.3
  37.7 0.8 broadcast_in_dim.8
  38.5 16.4 %all-to-all-done.1.refs_0_ = bf16[64,32,128]{2,1,0:T(8,128)(2,1)S(1)} async-done(((bf16[64,32,128]{2,1,0:T(8,128)(2,1)}), bf16[64,32,128]{2,1,0:T(8,128)(2,1)S(1)}, u32[]{:S(2)}, u32[]{:S(2)}) %all-to-all-start.1) | async-done | bytes 524320 | tf_op jit(solution)/shard_map/all_to_all | solution.py:194
  55.0 0.0 copy-start
  55.0 3.5 %all-to-all-start.3 = ((bf16[8,64,512]{2,1,0:T(8,128)(2,1)}), bf16[8,64,512]{2,1,0:T(8,128)(2,1)S(1)}, u32[]{:S(2)}, u32[]{:S(2)}) async-start(bf16[8,64,512]{2,1,0:T(8,128)(2,1)} %broadcast_in_dim.8), calls=%async_computation.3 | async-start | bytes 1048576 | tf_op jit(solution)/shard_map/all_to_all | solution.py:197
  58.5 0.0 copy-done
  58.5 2.5 %combine.1 = (f32[512,128]{1,0:T(8,128)}, f32[8,128]{1,0:T(8,128)}) custom-call(bf16[64,32,128]{2,1,0:T(8,128)(2,1)} %copy-done), custom_call_target="tpu_custom_call" | custom-call | tf_op jit(solution)/shard_map/combine/pallas_call | solution.py:143
  60.9 15.5 %all-to-all-done.3 = bf16[8,64,512]{2,1,0:T(8,128)(2,1)S(1)} async-done(((bf16[8,64,512]{2,1,0:T(8,128)(2,1)}), bf16[8,64,512]{2,1,0:T(8,128)(2,1)S(1)}, u32[]{:S(2)}, u32[]{:S(2)}) %all-to-all-start.3) | async-done | bytes 524320 | tf_op jit(solution)/shard_map/all_to_all | solution.py:197
  76.4 0.0 copy-start.1
  76.4 28.5 %all_to_all.25 = f32[512,1,128]{2,1,0:T(1,128)} all-to-all(f32[512,1,128]{2,1,0:T(1,128)} %bitcast.15), channel_id=1, replica_groups=mesh['graph'=64,'basis'=8] {'basis','graph'}, dimensions={0} | all-to-all | bytes 524288 | tf_op jit(solution)/shard_map/all_to_all | solution.py:203
  104.9 0.0 copy-done.1
  104.9 3.0 %edges.1 = (bf16[128,512]{1,0:T(8,128)(2,1)}, bf16[64,8,128]{2,1,0:T(8,128)(2,1)}) custom-call(f32[512,128]{1,0:T(8,128)} %bitcast.13, bf16[512,512]{1,0:T(8,128)(2,1)} %bitcast.12, bf16[128,512]{1,0:T(8,128)(2,1)} %edge_ref.3, bf16[512,512]{1,0:T(8,128)(2,1)} %first_ref.2, bf16[512,512]{1,0:T(8,128)(2,1)} %second_ref.2, f32[8,128]{1,0:T(8,128)} %get-tuple-element.9.head_ref), custom_call_target="tpu_custom_call" | custom-call | tf_op jit(solution)/shard_map/edges/pallas_call | solution.py:143
  107.9 15.8 %all_to_all.26.arrived_ref = bf16[64,8,128]{2,1,0:T(8,128)(2,1)} all-to-all(bf16[64,8,128]{2,1,0:T(8,128)(2,1)} %get-tuple-element.14), channel_id=1, replica_groups=mesh['graph'=64,'basis'=8] {'graph'}, dimensions={0} | all-to-all | bytes 262144 | tf_op jit(solution)/shard_map/all_to_all | solution.py:213
  123.7 2.4 %atoms.1 = bf16[32,512]{1,0:T(8,128)(2,1)} custom-call(bf16[64,8,128]{2,1,0:T(8,128)(2,1)} %all_to_all.26.arrived_ref, f32[8,128]{1,0:T(8,128)} %get-tuple-element.15.ids_ref, bf16[32,512]{1,0:T(8,128)(2,1)} %feats_ref.1, bf16[512,512]{1,0:T(8,128)(2,1)} %first_ref.3, bf16[512,512]{1,0:T(8,128)(2,1)} %second_ref.3), custom_call_target="tpu_custom_call" | custom-call | tf_op jit(solution)/shard_map/atoms/pallas_call | solution.py:143
Async XLA Ops:
  2.8 15.7 %all-to-all-start = ((bf16[8,64,128]{2,1,0:T(8,128)(2,1)}), bf16[8,64,128]{2,1,0:T(8,128)(2,1)S(1)}, u32[]{:S(2)}, u32[]{:S(2)}) async-start(bf16[8,64,128]{2,1,0:T(8,128)(2,1)} %lower.1), calls=%async_computation | async-start | bytes 262144 | tf_op jit(solution)/shard_map/all_to_all | solution.py:182
  18.5 0.7 copy-start.2
  22.2 15.5 %copy-start.3 = (bf16[1,64,512]{2,1,0:T(8,128)(2,1)S(1)}, bf16[1,64,512]{2,1,0:T(8,128)(2,1)}, u32[]{:S(2)}) copy-start(bf16[1,64,512]{2,1,0:T(8,128)(2,1)} %param.23) | copy-start | bytes 196612
  22.2 32.8 %all-to-all-start.1 = ((bf16[64,32,128]{2,1,0:T(8,128)(2,1)}), bf16[64,32,128]{2,1,0:T(8,128)(2,1)S(1)}, u32[]{:S(2)}, u32[]{:S(2)}) async-start(bf16[64,32,128]{2,1,0:T(8,128)(2,1)} %products.1), calls=%async_computation.1 | async-start | bytes 1048576 | tf_op jit(solution)/shard_map/all_to_all | solution.py:194
  55.0 3.5 %copy-start = (bf16[64,32,128]{2,1,0:T(8,128)(2,1)}, bf16[64,32,128]{2,1,0:T(8,128)(2,1)S(1)}, u32[]{:S(2)}) copy-start(bf16[64,32,128]{2,1,0:T(8,128)(2,1)S(1)} %all-to-all-done.1.refs_0_) | copy-start | bytes 1572868
  55.0 21.4 %all-to-all-start.3 = ((bf16[8,64,512]{2,1,0:T(8,128)(2,1)}), bf16[8,64,512]{2,1,0:T(8,128)(2,1)S(1)}, u32[]{:S(2)}, u32[]{:S(2)}) async-start(bf16[8,64,512]{2,1,0:T(8,128)(2,1)} %broadcast_in_dim.8), calls=%async_computation.3 | async-start | bytes 1048576 | tf_op jit(solution)/shard_map/all_to_all | solution.py:197
  76.4 28.5 %copy-start.1 = (bf16[8,64,512]{2,1,0:T(8,128)(2,1)}, bf16[8,64,512]{2,1,0:T(8,128)(2,1)S(1)}, u32[]{:S(2)}) copy-start(bf16[8,64,512]{2,1,0:T(8,128)(2,1)S(1)} %all-to-all-done.3) | copy-start | bytes 1572868

commit v2 on v1

--- a/solution.py
+++ b/solution.py
@@ -105,8 +105,19 @@
     out_ref[...] = total
 
 
-def edge_kernel(columns_ref, up_ref, edge_ref, first_ref, second_ref, head_ref, out_ref, send_ref, scratch):
-    triplet = dot(columns_ref[...].astype(bf16), up_ref[...], 0, 0)
+def edge_kernel(
+    peers, at_ref, columns_ref, up_ref, swapped_ref, edge_ref, first_ref, second_ref, head_ref, out_ref, send_ref, scratch
+):
+    core, group = at_ref[0], at_ref[1]
+    blocks = columns_ref.shape[0] // peers
+    half = up_ref.shape[0] // blocks
+    triplet = jnp.zeros(out_ref.shape, f32)
+    for side, ref in ((core, up_ref), (1 - core, swapped_ref)):
+        found = [
+            columns_ref[pl.ds(pl.multiple_of(((group ^ j) * 2 + side) * half, half), half), :]
+            for j in range(blocks)
+        ]
+        triplet = triplet + dot(jnp.concatenate(found, axis=0).astype(bf16), ref[...], 0, 0)
     joined = (edge_ref[...].astype(f32) + triplet).astype(bf16)
     inner = silu(dot(joined, first_ref[...], 1, 0)).astype(bf16)
     second = silu(dot(inner, second_ref[...], 1, 0))
@@ -139,14 +150,22 @@
     out_ref[...] = (feats_ref[...].astype(f32) + dot(hidden, second_ref[...], 1, 0)).astype(bf16)
 
 
-def call(kernel, name, specs, outs, *args, scratch=()):
+def call(kernel, name, specs, outs, *args, scratch=(), keep=(), pinned=True):
+    args = [
+        pltpu.with_memory_space_constraint(a, pltpu.VMEM) if pinned and s is VMEM else a
+        for a, s in zip(args, specs)
+    ]
     return pl.pallas_call(
         kernel,
         name=name,
         in_specs=specs,
         out_specs=[VMEM] * len(outs),
-        out_shape=[jax.ShapeDtypeStruct(shape, dtype) for shape, dtype in outs],
+        out_shape=[
+            jax.ShapeDtypeStruct(shape, dtype) if i in keep else pltpu.VMEM(shape, dtype)
+            for i, (shape, dtype) in enumerate(outs)
+        ],
         scratch_shapes=scratch,
+        compiler_params=pltpu.CompilerParams(vmem_limit_bytes=16 << 20),
     )(*args)
 
 
@@ -177,7 +196,7 @@
 
     (lowered,) = call(
         lower_kernel, "lower", [VMEM] * 3, [((blocks, narrow, rows), bf16)],
-        edge_feats, pre_weight, down_weight.T,
+        edge_feats, pre_weight, down_weight.T, pinned=False,
     )
     lowered = lax.all_to_all(lowered, "basis", 0, 0, tiled=True)
     head, atoms = call(
@@ -192,9 +211,16 @@
         scratch=[pltpu.VMEM((peers * packed, 128), f32)],
     )
     arrived = lax.all_to_all(send, "graph", 0, 0, tiled=True)
-    ups = jnp.broadcast_to(up_weight, (blocks, narrow, width))
-    ups, _ = lax.optimization_barrier((ups, send))
-    ups = lax.all_to_all(ups, "basis", 0, 0, tiled=True)
+    core = lax.axis_index("graph") % 2
+    half = narrow // 2
+    ups = lax.dynamic_slice_in_dim(up_weight[0], core * half, half, 0)
+    ups, _ = lax.optimization_barrier((ups, lowered))
+    step = 1
+    while step < blocks:
+        other = lax.ppermute(ups, "basis", [(j, j ^ step) for j in range(blocks)])
+        ups = jnp.concatenate([ups, other], axis=0)
+        step *= 2
+    swapped = lax.ppermute(ups, "graph", [(j, j ^ 1) for j in range(peers)])
     summed, ids = call(
         lambda *refs: combine_kernel(parts, blocks, *refs), "combine", [VMEM],
         [((peers * blocks, 128), f32), ((packed - parts, 128), f32)],
@@ -204,16 +230,17 @@
         summed.reshape(peers * blocks, 1, 128), ("basis", "graph"), 0, 0, tiled=True
     )
     edge_update, send = call(
-        edge_kernel, "edges", [VMEM] * 6,
+        lambda *refs: edge_kernel(peers, *refs), "edges", [SMEM] + [VMEM] * 7,
         [((rows, width), bf16), ((peers, 2 * width // 128, 128), bf16)],
-        columns.reshape(peers * blocks, 128), ups.reshape(blocks * narrow, width), edge_feats,
-        res_first, res_second, head,
+        jnp.stack([core, lax.axis_index("basis")]).astype(i32),
+        columns.reshape(peers * blocks, 128), ups, swapped, edge_feats,
+        res_first, res_second, head, keep=(0,),
         scratch=[pltpu.VMEM((peers * 2 * width // 128, 128), f32)],
     )
     arrived = lax.all_to_all(send, "graph", 0, 0, tiled=True)
     (atom_update,) = call(
         atom_kernel, "atoms", [VMEM] * 5, [(atom_feats.shape, bf16)],
-        arrived, ids, atom_feats, atom_first, atom_second,
+        arrived, ids, atom_feats, atom_first, atom_second, keep=(0,),
         scratch=[pltpu.VMEM((peers * 2 * width // 128, 128), f32)],
     )
     return (edge_update, atom_update)

time: 127 us -> 110 us (0.87)
  blocking collectives: 44.3 us -> 15.4 us
  starting transfers between devices: 26.6 us -> 51 us
  waiting for transfers between devices: 38.4 us -> 29.3 us
  Pallas kernels: 14.6 us -> 8.18 us
  local copies, waits for them, and re-layouts: 1.51 us -> 4.26 us
    all_to_all x1 -> x0, blocking collectives: 28.5 us -> none  [body(): lax.all_to_all(summed.reshape(peers * blocks, 1, 128), ('basis', 'graph')...]
    all_to_all x1, waiting for transfers between devices: 16.4 us -> 3.65 us  [body(): arrived = lax.all_to_all(send, 'graph', 0, 0, tiled=True)]
    all_to_all x1, starting transfers between devices: 3.49 us -> 15.8 us  [body(): lax.all_to_all(summed.reshape(peers * blocks, 1, 128), ('basis', 'graph')...]
    ppermute x0 -> x4, starting transfers between devices: none -> 12.2 us  [the longest x1 6.34 us: body(): swapped = lax.ppermute(ups, 'graph', [(j, j ^ 1) for j in range(peers)])]
    ppermute x0 -> x4, waiting for transfers between devices: none -> 8.78 us  [the longest x3 7.72 us: body(): other = lax.ppermute(ups, 'basis', [(j, j ^ step) for j in range(blocks)])]
    pallas_call x6, Pallas kernels: 14.6 us -> 8.18 us  [call(): pl.pallas_call(kernel, name=name, in_specs=specs, out_specs=[VMEM] * len(...]
    all_to_all x1, waiting for transfers between devices: 15.5 us -> 9.78 us  [body(): lax.all_to_all(summed.reshape(peers * blocks, 1, 128), ('basis', 'graph')...]
    unnamed x8 -> x37, local copies, waits for them, and re-layouts: 0.67 us -> 4.24 us
  transfers between devices with their start and end apart: 3 -> 7, of which waited for: 3 -> 6; matrix products, arithmetic and copies ran while one was open for 1% -> 0% of each run, Pallas kernels for 3% -> 1%
where the time goes in v2:
time: 110 us; the launch traced here: 109 us
  starting transfers between devices  51 us (46%)
  waiting for transfers between devices  29.3 us (27%)
  blocking collectives  15.4 us (14%)
  Pallas kernels  8.18 us (7%)
  local copies, waits for them, and re-layouts  4.26 us (4%)
    all_to_all x1, starting transfers between devices, body(): lax.all_to_all(summed.reshape(peers * blocks, 1, 128), ('basis', 'graph')...  15.8 us
    all_to_all x1, blocking collectives, body(): arrived = lax.all_to_all(send, 'graph', 0, 0, tiled=True)  15.4 us
    all_to_all x1, starting transfers between devices, body(): arrived = lax.all_to_all(send, 'graph', 0, 0, tiled=True)  15.4 us
    all_to_all x1, waiting for transfers between devices, body(): lax.all_to_all(summed.reshape(peers * blocks, 1, 128), ('basis', 'graph')...  9.78 us
    pallas_call x6, Pallas kernels, call(): pl.pallas_call(kernel, name=name, in_specs=specs, out_specs=[VMEM] * len(...  8.18 us
    ppermute x3, waiting for transfers between devices, body(): other = lax.ppermute(ups, 'basis', [(j, j ^ step) for j in range(blocks)])  7.72 us
    all_to_all x1, starting transfers between devices, body(): lowered = lax.all_to_all(lowered, 'basis', 0, 0, tiled=True)  7.64 us
    all_to_all x1, waiting for transfers between devices, body(): lowered = lax.all_to_all(lowered, 'basis', 0, 0, tiled=True)  7.1 us
  transfers between devices with their start and end apart: 7, of which 6 were waited for; matrix products, arithmetic and copies ran while one was open for 0% of the time, Pallas kernels for 1%

profile of v2, /device:TPU:1, one launch (start us, length us, event | category | flops | bytes accessed | tf_op | source)
XLA Modules:
  0.0 109.1 jit_solution(4020538347670356689)
XLA Ops:
  0.6 0.0 copy-start
  0.6 0.0 copy-start.1
  0.7 0.0 copy-start.6
  0.7 1.0 copy-done.6
  1.6 0.0 copy-start.8
  1.6 1.0 copy-done.8
  2.7 0.0 copy-start.9
  2.7 0.8 copy-done.9
  3.5 1.1 %lower.1 = bf16[8,64,128]{2,1,0:T(8,128)(2,1)} custom-call(bf16[128,512]{1,0:T(8,128)(2,1)S(1)} %copy-done.6, bf16[512,512]{1,0:T(8,128)(2,1)S(1)} %copy-done.8, bf16[64,512]{1,0:T(8,128)(2,1)S(1)} %bitcast.16), custom_call_target="tpu_custom_call" | custom-call | tf_op jit(solution)/shard_map/lower/pallas_call | solution.py:158
  4.6 7.6 %all-to-all-start = ((bf16[8,64,128]{2,1,0:T(8,128)(2,1)}), bf16[8,64,128]{2,1,0:T(8,128)(2,1)S(1)}, u32[]{:S(2)}, u32[]{:S(2)}) async-start(bf16[8,64,128]{2,1,0:T(8,128)(2,1)} %lower.1), calls=%async_computation | async-start | bytes 262144 | tf_op jit(solution)/shard_map/all_to_all | solution.py:201
  12.3 0.0 copy-start.15
  12.3 0.0 copy-start.16
  12.3 0.0 copy-start.12
  12.3 0.0 copy-start.13
  12.3 0.0 copy-start.14
  12.3 0.6 copy-done.15
  12.9 0.0 copy-done.16
  12.9 0.0 copy-done.12
  12.9 0.0 copy-done.13
  13.0 0.0 copy-done.14
  13.0 0.2 tables.1
  13.2 7.1 %all-to-all-done.lowered_ref = bf16[8,64,128]{2,1,0:T(8,128)(2,1)S(1)} async-done(((bf16[8,64,128]{2,1,0:T(8,128)(2,1)}), bf16[8,64,128]{2,1,0:T(8,128)(2,1)S(1)}, u32[]{:S(2)}, u32[]{:S(2)}) %all-to-all-start) | async-done | bytes 131104 | tf_op jit(solution)/shard_map/all_to_all | solution.py:201
  20.3 0.0 copy-start.11
  20.3 0.0 copy-done.1
  20.3 0.7 copy-done.11
  20.9 2.4 %products.1 = bf16[64,32,128]{2,1,0:T(8,128)(2,1)} custom-call(s32[24]{0:T(128)S(1)} %copy-done.11, bf16[8,64,128]{2,1,0:T(8,128)(2,1)S(1)} %all-to-all-done.lowered_ref, bf16[24,128,128]{2,1,0:T(8,128)(2,1)S(1)} %bitcast.15, f32[8,128]{1,0:T(8,128)S(1)} %get-tuple-element.9.head_ref.refs_7_, f32[64,128]{1,0:T(8,128)S(1)} %get-tuple-element.10.atoms_ref), custom_call_target="tpu_custom_call" | custom-call | tf_op jit(solution)/shard_map/products/pallas_call | solution.py:158
  23.4 15.4 %all-to-all-start.1 = ((bf16[64,32,128]{2,1,0:T(8,128)(2,1)}), bf16[64,32,128]{2,1,0:T(8,128)(2,1)S(1)}, u32[]{:S(2)}, u32[]{:S(2)}) async-start(bf16[64,32,128]{2,1,0:T(8,128)(2,1)} %products.1), calls=%async_computation.1 | async-start | bytes 1048576 | tf_op jit(solution)/shard_map/all_to_all | solution.py:213
  38.8 0.0 copy-done
  38.8 2.0 %collective-permute-start = (bf16[32,512]{1,0:T(8,128)(2,1)S(1)}, bf16[32,512]{1,0:T(8,128)(2,1)S(1)}, u32[]{:S(2)}, u32[]{:S(2)}) collective-permute-start(bf16[32,512]{1,0:T(8,128)(2,1)S(1)} %dynamic-slice_bitcast_fusion), channel_id=1, source_target_pairs={{0,1},{1,0},{2,3},{3,2},{4,5},{5,4},{6,7},{7,6},{8,9},{9,8},{10,11... | collective-permute-start | bytes 98312 | tf_op jit(solution)/shard_map/ppermute | solution.py:220
  40.8 3.0 %collective-permute-done = bf16[32,512]{1,0:T(8,128)(2,1)S(1)} collective-permute-done((bf16[32,512]{1,0:T(8,128)(2,1)S(1)}, bf16[32,512]{1,0:T(8,128)(2,1)S(1)}, u32[]{:S(2)}, u32[]{:S(2)}) %collective-permute-start) | collective-permute-done | bytes 32800 | tf_op jit(solution)/shard_map/ppermute | solution.py:220
  43.8 1.9 %collective-permute-start.1 = (bf16[64,512]{1,0:T(8,128)(2,1)S(1)}, bf16[64,512]{1,0:T(8,128)(2,1)S(1)}, u32[]{:S(2)}, u32[]{:S(2)}) collective-permute-start(bf16[64,512]{1,0:T(8,128)(2,1)S(1)} %pad_maximum_fusion.1), channel_id=1, source_target_pairs={{0,2},{1,3},{2,0},{3,1},{4,6},{5,7},{6,4},{7,5},{8,10},{9,11},{10,... | collective-permute-start | bytes 196616 | tf_op jit(solution)/shard_map/ppermute | solution.py:220
  45.7 4.8 %collective-permute-done.1 = bf16[64,512]{1,0:T(8,128)(2,1)S(1)} collective-permute-done((bf16[64,512]{1,0:T(8,128)(2,1)S(1)}, bf16[64,512]{1,0:T(8,128)(2,1)S(1)}, u32[]{:S(2)}, u32[]{:S(2)}) %collective-permute-start.1) | collective-permute-done | bytes 65568 | tf_op jit(solution)/shard_map/ppermute | solution.py:220
  50.5 1.9 %collective-permute-start.2 = (bf16[128,512]{1,0:T(8,128)(2,1)S(1)}, bf16[128,512]{1,0:T(8,128)(2,1)S(1)}, u32[]{:S(2)}, u32[]{:S(2)}) collective-permute-start(bf16[128,512]{1,0:T(8,128)(2,1)S(1)} %pad_maximum_fusion), channel_id=1, source_target_pairs={{0,4},{1,5},{2,6},{3,7},{4,0},{5,1},{6,2},{7,3},{8,12},{9,13},{10,... | collective-permute-start | bytes 393224 | tf_op jit(solution)/shard_map/ppermute | solution.py:220
  52.4 3.6 %all-to-all-done.1.refs_0_ = bf16[64,32,128]{2,1,0:T(8,128)(2,1)S(1)} async-done(((bf16[64,32,128]{2,1,0:T(8,128)(2,1)}), bf16[64,32,128]{2,1,0:T(8,128)(2,1)S(1)}, u32[]{:S(2)}, u32[]{:S(2)}) %all-to-all-start.1) | async-done | bytes 524320 | tf_op jit(solution)/shard_map/all_to_all | solution.py:213
  56.0 0.0 copy-start.3
  56.1 1.4 %combine.1 = (f32[512,128]{1,0:T(8,128)}, f32[8,128]{1,0:T(8,128)S(1)}) custom-call(bf16[64,32,128]{2,1,0:T(8,128)(2,1)S(1)} %all-to-all-done.1.refs_0_), custom_call_target="tpu_custom_call" | custom-call | tf_op jit(solution)/shard_map/combine/pallas_call | solution.py:158
  57.5 0.0 copy-start.2
  57.5 15.8 %all-to-all-start.2 = ((f32[512,1,128]{2,1,0:T(1,128)}), f32[512,1,128]{2,1,0:T(1,128)S(1)}, u32[]{:S(2)}, u32[]{:S(2)}) async-start(f32[512,1,128]{2,1,0:T(1,128)} %bitcast.9), calls=%async_computation.2 | async-start | bytes 524288 | tf_op jit(solution)/shard_map/all_to_all | solution.py:229
  73.3 0.0 copy-start.7
  73.3 0.0 collective-permute-done.2
  73.4 6.3 %collective-permute-start.3 = (bf16[256,512]{1,0:T(8,128)(2,1)S(1)}, bf16[256,512]{1,0:T(8,128)(2,1)S(1)}, u32[]{:S(2)}, u32[]{:S(2)}) collective-permute-start(bf16[256,512]{1,0:T(8,128)(2,1)S(1)} %constant_dynamic-update-slice_fusion.refs_2_), channel_id=1, source_target_pairs={{0,8},{8,0},{16,24},{24,16},{32,40},{40,32},{48,56},{56,48},{64,72... | collective-permute-start | bytes 786440 | tf_op jit(solution)/shard_map/ppermute | solution.py:223
  79.7 0.1 pad_add_fusion.refs_0_
  79.8 1.1 collective-permute-done.3.refs_3_
  80.9 9.8 %all-to-all-done.2 = f32[512,1,128]{2,1,0:T(1,128)S(1)} async-done(((f32[512,1,128]{2,1,0:T(1,128)}), f32[512,1,128]{2,1,0:T(1,128)S(1)}, u32[]{:S(2)}, u32[]{:S(2)}) %all-to-all-start.2) | async-done | bytes 262176 | tf_op jit(solution)/shard_map/all_to_all | solution.py:229
  90.6 0.0 copy-done.3
  90.6 0.0 copy-done.2
  90.6 0.0 copy-done.7
  90.6 0.0 copy-start.4
  90.7 0.0 copy-start.5
  90.7 1.9 %edges.1 = (bf16[128,512]{1,0:T(8,128)(2,1)}, bf16[64,8,128]{2,1,0:T(8,128)(2,1)S(1)}) custom-call(s32[2]{0:T(128)S(1)} %pad_add_fusion.refs_0_, f32[512,128]{1,0:T(8,128)S(1)} %bitcast.14, bf16[256,512]{1,0:T(8,128)(2,1)S(1)} %constant_dynamic-update-slice_fusion.refs_2_, bf16[256,512]{1,0:T(8,128)(2,1)S(1)} %collective-permute-done.3.refs_3_, ...), custom_call_target="tpu_custom_call" | custom-call | tf_op jit(solution)/shard_map/edges/pallas_call | solution.py:158
  92.6 0.0 copy-start.10
  92.6 15.4 %all_to_all.20.arrived_ref = bf16[64,8,128]{2,1,0:T(8,128)(2,1)S(1)} all-to-all(bf16[64,8,128]{2,1,0:T(8,128)(2,1)S(1)} %get-tuple-element.14), channel_id=1, replica_groups=mesh['graph'=64,'basis'=8] {'graph'}, dimensions={0} | all-to-all | bytes 262144 | tf_op jit(solution)/shard_map/all_to_all | solution.py:240
  108.0 0.0 copy-done.4
  108.0 0.0 copy-done.5
  108.0 0.0 copy-done.10
  108.0 1.1 %atoms.1 = bf16[32,512]{1,0:T(8,128)(2,1)} custom-call(bf16[64,8,128]{2,1,0:T(8,128)(2,1)S(1)} %all_to_all.20.arrived_ref, f32[8,128]{1,0:T(8,128)S(1)} %get-tuple-element.15.ids_ref, bf16[32,512]{1,0:T(8,128)(2,1)S(1)} %copy-done.10, bf16[512,512]{1,0:T(8,128)(2,1)S(1)} %copy-done.4, bf16[512,512]{1,0:T(8,128)(2,1)S(1)} %copy-done.5), custom_call_target="tpu_custom_call" | custom-call | tf_op jit(solution)/shard_map/atoms/pallas_call | solution.py:158
  (7 shorter events, 0.1 us)
Async XLA Ops:
  0.6 38.1 %copy-start = (bf16[1,64,512]{2,1,0:T(8,128)(2,1)S(1)}, bf16[1,64,512]{2,1,0:T(8,128)(2,1)}, u32[]{:S(2)}) copy-start(bf16[1,64,512]{2,1,0:T(8,128)(2,1)} %param.23) | copy-start | bytes 196612
  0.6 19.6 %copy-start.1 = (bf16[24,1,128,128]{3,2,1,0:T(8,128)(2,1)S(1)}, bf16[24,1,128,128]{3,2,1,0:T(8,128)(2,1)}, u32[]{:S(2)}) copy-start(bf16[24,1,128,128]{3,2,1,0:T(8,128)(2,1)} %param.19) | copy-start | bytes 2359300
  0.7 1.0 copy-start.6
  1.6 1.0 copy-start.8
  2.7 0.8 copy-start.9
  4.6 15.7 %all-to-all-start = ((bf16[8,64,128]{2,1,0:T(8,128)(2,1)}), bf16[8,64,128]{2,1,0:T(8,128)(2,1)S(1)}, u32[]{:S(2)}, u32[]{:S(2)}) async-start(bf16[8,64,128]{2,1,0:T(8,128)(2,1)} %lower.1), calls=%async_computation | async-start | bytes 262144 | tf_op jit(solution)/shard_map/all_to_all | solution.py:201
  12.3 0.7 copy-start.15
  12.3 0.7 copy-start.16
  12.3 0.7 copy-start.12
  12.3 0.7 copy-start.13
  12.3 0.7 copy-start.14
  20.3 0.7 copy-start.11
  23.4 32.7 %all-to-all-start.1 = ((bf16[64,32,128]{2,1,0:T(8,128)(2,1)}), bf16[64,32,128]{2,1,0:T(8,128)(2,1)S(1)}, u32[]{:S(2)}, u32[]{:S(2)}) async-start(bf16[64,32,128]{2,1,0:T(8,128)(2,1)} %products.1), calls=%async_computation.1 | async-start | bytes 1048576 | tf_op jit(solution)/shard_map/all_to_all | solution.py:213
  38.8 5.0 %collective-permute-start = (bf16[32,512]{1,0:T(8,128)(2,1)S(1)}, bf16[32,512]{1,0:T(8,128)(2,1)S(1)}, u32[]{:S(2)}, u32[]{:S(2)}) collective-permute-start(bf16[32,512]{1,0:T(8,128)(2,1)S(1)} %dynamic-slice_bitcast_fusion), channel_id=1, source_target_pairs={{0,1},{1,0},{2,3},{3,2},{4,5},{5,4},{6,7},{7,6},{8,9},{9,8},{10,11... | collective-permute-start | bytes 98312 | tf_op jit(solution)/shard_map/ppermute | solution.py:220
  43.8 6.7 %collective-permute-start.1 = (bf16[64,512]{1,0:T(8,128)(2,1)S(1)}, bf16[64,512]{1,0:T(8,128)(2,1)S(1)}, u32[]{:S(2)}, u32[]{:S(2)}) collective-permute-start(bf16[64,512]{1,0:T(8,128)(2,1)S(1)} %pad_maximum_fusion.1), channel_id=1, source_target_pairs={{0,2},{1,3},{2,0},{3,1},{4,6},{5,7},{6,4},{7,5},{8,10},{9,11},{10,... | collective-permute-start | bytes 196616 | tf_op jit(solution)/shard_map/ppermute | solution.py:220
  50.5 22.9 %collective-permute-start.2 = (bf16[128,512]{1,0:T(8,128)(2,1)S(1)}, bf16[128,512]{1,0:T(8,128)(2,1)S(1)}, u32[]{:S(2)}, u32[]{:S(2)}) collective-permute-start(bf16[128,512]{1,0:T(8,128)(2,1)S(1)} %pad_maximum_fusion), channel_id=1, source_target_pairs={{0,4},{1,5},{2,6},{3,7},{4,0},{5,1},{6,2},{7,3},{8,12},{9,13},{10,... | collective-permute-start | bytes 393224 | tf_op jit(solution)/shard_map/ppermute | solution.py:220
  56.0 34.6 %copy-start.3 = (bf16[512,512]{1,0:T(8,128)(2,1)S(1)}, bf16[512,512]{1,0:T(8,128)(2,1)}, u32[]{:S(2)}) copy-start(bf16[512,512]{1,0:T(8,128)(2,1)} %refs_6_.1) | copy-start | bytes 1572868
  57.5 33.2 %copy-start.2 = (bf16[512,512]{1,0:T(8,128)(2,1)S(1)}, bf16[512,512]{1,0:T(8,128)(2,1)}, u32[]{:S(2)}) copy-start(bf16[512,512]{1,0:T(8,128)(2,1)} %refs_5_.1) | copy-start | bytes 1572868
  57.5 33.2 %all-to-all-start.2 = ((f32[512,1,128]{2,1,0:T(1,128)}), f32[512,1,128]{2,1,0:T(1,128)S(1)}, u32[]{:S(2)}, u32[]{:S(2)}) async-start(f32[512,1,128]{2,1,0:T(1,128)} %bitcast.9), calls=%async_computation.2 | async-start | bytes 524288 | tf_op jit(solution)/shard_map/all_to_all | solution.py:229
  73.3 17.3 %copy-start.7 = (bf16[128,512]{1,0:T(8,128)(2,1)S(1)}, bf16[128,512]{1,0:T(8,128)(2,1)}, u32[]{:S(2)}) copy-start(bf16[128,512]{1,0:T(8,128)(2,1)} %refs_4_.1) | copy-start | bytes 393220
  73.4 7.5 %collective-permute-start.3 = (bf16[256,512]{1,0:T(8,128)(2,1)S(1)}, bf16[256,512]{1,0:T(8,128)(2,1)S(1)}, u32[]{:S(2)}, u32[]{:S(2)}) collective-permute-start(bf16[256,512]{1,0:T(8,128)(2,1)S(1)} %constant_dynamic-update-slice_fusion.refs_2_), channel_id=1, source_target_pairs={{0,8},{8,0},{16,24},{24,16},{32,40},{40,32},{48,56},{56,48},{64,72... | collective-permute-start | bytes 786440 | tf_op jit(solution)/shard_map/ppermute | solution.py:223
  90.6 17.4 %copy-start.4 = (bf16[512,512]{1,0:T(8,128)(2,1)S(1)}, bf16[512,512]{1,0:T(8,128)(2,1)}, u32[]{:S(2)}) copy-start(bf16[512,512]{1,0:T(8,128)(2,1)} %first_ref.1) | copy-start | bytes 1572868
  90.7 17.4 %copy-start.5 = (bf16[512,512]{1,0:T(8,128)(2,1)S(1)}, bf16[512,512]{1,0:T(8,128)(2,1)}, u32[]{:S(2)}) copy-start(bf16[512,512]{1,0:T(8,128)(2,1)} %second_ref.1) | copy-start | bytes 1572868
  92.6 15.4 %copy-start.10 = (bf16[32,512]{1,0:T(8,128)(2,1)S(1)}, bf16[32,512]{1,0:T(8,128)(2,1)}, u32[]{:S(2)}) copy-start(bf16[32,512]{1,0:T(8,128)(2,1)} %feats_ref.1) | copy-start | bytes 98308

commit v3 on v2

v3 whole, which is shorter than its diff:
```python
import jax
import jax.numpy as jnp
from jax import lax
from jax.experimental import pallas as pl
from jax.experimental.pallas import tpu as pltpu
from jax.sharding import PartitionSpec as P

half_root = 0.5**0.5
f32, bf16, i32 = jnp.float32, jnp.bfloat16, jnp.int32
VMEM = pl.BlockSpec(memory_space=pltpu.VMEM)
SMEM = pl.BlockSpec(memory_space=pltpu.SMEM)
GRAPH = ("x", "z", "core")
HEAD = 8
OFFSET = 256


def iota(shape, axis):
    return lax.broadcasted_iota(i32, shape, axis)


def silu(v):
    return v / (1.0 + jnp.exp(-v))


def dot(a, b, left, right):
    return lax.dot_general(a, b, (((left,), (right,)), ((), ())), preferred_element_type=f32)


def lower_kernel(z_size, edge_ref, pre_ref, down_ref, out_ref):
    projected = silu(dot(edge_ref[...], pre_ref[...], 1, 0)).astype(bf16)
    lowered = silu(dot(down_ref[...], projected, 1, 1)).astype(bf16)
    narrow = lowered.shape[0]
    to, at = iota((narrow, narrow), 0), iota((narrow, narrow), 1)
    feature = (to // 2 % z_size) * (narrow // z_size) + to // (2 * z_size) * 2 + to % 2
    order = jnp.where(at == feature, 1.0, 0.0).astype(bf16)
    lowered = dot(order, lowered, 1, 0).astype(bf16)
    for i in range(out_ref.shape[0]):
        out_ref[i] = lowered


def column(row):
    n = row.shape[1]
    return jnp.sum(jnp.where(iota((n, n), 0) == iota((n, n), 1), row, 0), axis=1, keepdims=True)


def table_kernel(sizes, me_ref, owner_ref, target_ref, slot_ref, slot_owner_ref, slot_atom_ref, head_ref, atoms_ref):
    me = me_ref[0]
    parts = owner_ref.shape[1]
    slots = slot_owner_ref.shape[1]
    rows = slot_ref.shape[1]
    owner = column(owner_ref[...])
    z_size, blocks = sizes
    x, z, core = owner // (2 * z_size), (owner // 2) % z_size, owner % 2
    ids = ((x * 2 + core) * blocks + column(target_ref[...])) * z_size + z - OFFSET
    place = iota((parts, 128), 1) == (iota((parts, 128), 0) + me * (parts + 2)) % 128
    id_row = jnp.sum(jnp.where(place, ids, 0), axis=0, keepdims=True)
    own_row = slot_owner_ref[...]
    own_col = column(own_row)
    same = own_col == own_row
    down, right = iota((slots, slots), 0), iota((slots, slots), 1)
    rank_row = jnp.sum(jnp.where(same & (down < right), 1, 0), axis=0, keepdims=True)
    rank_col = jnp.sum(jnp.where(same & (right < down), 1, 0), axis=1, keepdims=True)
    spot_col = own_col * 2 + rank_col
    spot_row = jnp.sum(
        jnp.where(slot_ref[...] == iota((slots, rows), 0), spot_col, 0), axis=0, keepdims=True
    )
    sub = iota((HEAD, 128), 0)
    head_ref[...] = jnp.where(sub == 0, id_row, jnp.where(sub == 1, spot_row, 0)).astype(f32)
    peers = atoms_ref.shape[0]
    atom = slot_atom_ref[...] + 1
    mine = iota((peers, slots), 0) == own_row
    first = jnp.sum(jnp.where(mine & (rank_row == 0), atom, 0), axis=1, keepdims=True)
    second = jnp.sum(jnp.where(mine & (rank_row == 1), atom, 0), axis=1, keepdims=True)
    lane = iota((peers, 128), 1)
    atoms = jnp.where(lane == 2 * me, first, jnp.where(lane == 2 * me + 1, second, 0))
    atoms_ref[...] = atoms.astype(f32)


def product_kernel(source_ref, lowered_ref, tiles_ref, head_ref, atoms_ref, out_ref, scratch):
    parts = tiles_ref.shape[0]
    peers = atoms_ref.shape[0]
    rows = parts + 2
    for p in range(parts):
        product = dot(lowered_ref[source_ref[p]], tiles_ref[p], 1, 1)
        scratch[pl.ds(p, peers, stride=rows), :] = product
    scratch[pl.ds(parts, peers, stride=rows), :] = jnp.broadcast_to(head_ref[0:1, :], (peers, 128))
    scratch[pl.ds(parts + 1, peers, stride=rows), :] = atoms_ref[...]
    out_ref[...] = scratch[...].astype(bf16)


def combine_kernel(parts, peers, arrived_ref, out_ref, atoms_ref, scratch):
    rows = parts + 2
    targets = out_ref.shape[0]
    scratch[...] = arrived_ref[...].astype(f32)
    heads = scratch[pl.ds(parts, peers, stride=rows), :]
    atoms = jnp.sum(scratch[pl.ds(parts + 1, peers, stride=rows), :], axis=0, keepdims=True)
    atoms_ref[...] = jnp.broadcast_to(atoms, atoms_ref.shape)
    source = iota((peers, 128), 0)
    row = iota((targets, 128), 0).astype(f32)
    chunks = peers * rows // 128
    total = jnp.zeros((targets, 128), f32)
    for r in range(0, chunks, 2):
        hits = []
        for q in range(r, min(r + 2, chunks)):
            item = iota((1, 128), 1) + q * 128
            ids = jnp.sum(jnp.where(source == item // rows, heads, 0.0), axis=0, keepdims=True)
            ids = jnp.where(item % rows < parts, ids + float(OFFSET), -1.0)
            hits.append(jnp.where(row == ids, 1.0, 0.0).astype(bf16))
        items = arrived_ref[r * 128 : (r + len(hits)) * 128, :]
        total = total + dot(jnp.concatenate(hits, axis=1), items, 1, 0)
    out_ref[...] = total.astype(bf16)


def edge_kernel(
    peers, at_ref, columns_ref, up_ref, swapped_ref, edge_ref, first_ref, second_ref, head_ref, out_ref, send_ref, scratch
):
    core, group = at_ref[0], at_ref[1]
    blocks = columns_ref.shape[0] // peers
    half = up_ref.shape[0] // blocks
    triplet = jnp.zeros(out_ref.shape, f32)
    for side, ref in ((core, up_ref), (1 - core, swapped_ref)):
        found = [
            columns_ref[pl.ds(pl.multiple_of(((group ^ j) * 2 + side) * half, half), half), :]
            for j in range(blocks)
        ]
        triplet = triplet + dot(jnp.concatenate(found, axis=0).astype(bf16), ref[...], 0, 0)
    joined = (edge_ref[...].astype(f32) + triplet).astype(bf16)
    inner = silu(dot(joined, first_ref[...], 1, 0)).astype(bf16)
    second = silu(dot(inner, second_ref[...], 1, 0))
    update = ((joined.astype(f32) + second) * half_root).astype(bf16)
    out_ref[...] = update
    places = send_ref.shape[0] * 2
    chunks = update.shape[1] // 128
    spot = iota((places, update.shape[0]), 0).astype(f32) == head_ref[1:2, :]
    sums = dot(jnp.where(spot, 1.0, 0.0).astype(bf16), update, 1, 0)
    for c in range(chunks):
        scratch[pl.ds(c, places, stride=chunks), :] = sums[:, c * 128 : (c + 1) * 128]
    send_ref[...] = scratch[...].reshape(send_ref.shape).astype(bf16)


def atom_kernel(arrived_ref, ids_ref, feats_ref, first_ref, second_ref, out_ref, scratch):
    places = arrived_ref.shape[0] * 2
    count, width = feats_ref.shape
    chunks = width // 128
    scratch[...] = arrived_ref[...].astype(f32).reshape(scratch.shape)
    hit = (iota((count, places), 0) + 1).astype(f32) == ids_ref[0:1, :]
    hit = jnp.where(hit, 1.0, 0.0).astype(bf16)
    gathered = jnp.concatenate(
        [
            dot(hit, scratch[pl.ds(c, places, stride=chunks), :].astype(bf16), 1, 0)
            for c in range(chunks)
        ],
        axis=1,
    ).astype(bf16)
    hidden = silu(dot(gathered, first_ref[...], 1, 0)).astype(bf16)
    out_ref[...] = (feats_ref[...].astype(f32) + dot(hidden, second_ref[...], 1, 0)).astype(bf16)


def call(kernel, name, specs, outs, *args, scratch=(), keep=(), space=pltpu.VMEM):
    args = [
        pltpu.with_memory_space_constraint(a, space) if s is VMEM else a
        for a, s in zip(args, specs)
    ]
    return pl.pallas_call(
        kernel,
        name=name,
        in_specs=specs,
        out_specs=[VMEM] * len(outs),
        out_shape=[
            jax.ShapeDtypeStruct(shape, dtype) if i in keep else pltpu.VMEM(shape, dtype)
            for i, (shape, dtype) in enumerate(outs)
        ],
        scratch_shapes=scratch,
        compiler_params=pltpu.CompilerParams(vmem_limit_bytes=16 << 20),
    )(*args)


def body(
    edge_feats,
    pre_weight,
    down_weight,
    angle_tiles,
    part_source,
    part_owner,
    part_target,
    up_weight,
    res_first,
    res_second,
    edge_slot,
    slot_owner,
    slot_atom,
    atom_feats,
    atom_first,
    atom_second,
):
    z_size, blocks = lax.axis_size("z"), lax.axis_size("basis")
    peers = lax.axis_size(GRAPH)
    parts = part_source.shape[0]
    narrow = down_weight.shape[1]
    rows, width = edge_feats.shape
    packed = parts + 2
    near = peers // z_size
    me = lax.axis_index(GRAPH).astype(i32).reshape(1)
    core, group = lax.axis_index("core"), lax.axis_index("basis")
    half = narrow // 2

    (lowered,) = call(
        lambda *refs: lower_kernel(z_size, *refs), "lower", [VMEM] * 3, [((blocks, narrow, rows), bf16)],
        edge_feats, pre_weight, down_weight.T, space=pltpu.HBM,
    )
    lowered, ups = lax.optimization_barrier((lowered, up_weight))
    ups = lax.dynamic_slice_in_dim(ups[0], core * half, half, 0)
    lowered = lax.all_to_all(lowered, "basis", 0, 0, tiled=True)
    other = lax.ppermute(ups, "basis", [(j, j ^ 1) for j in range(blocks)])
    lowered, other = lax.optimization_barrier((lowered, other))
    head, atoms = call(
        lambda *refs: table_kernel((z_size, blocks), *refs), "tables", [SMEM] + [VMEM] * 5,
        [((HEAD, 128), f32), ((peers, 128), f32)],
        me, part_owner.reshape(1, parts), part_target.reshape(1, parts), edge_slot,
        slot_owner.reshape(1, -1), slot_atom,
    )
    source = jnp.clip(part_source, 0, blocks - 1)
    (send,) = call(
        product_kernel, "products", [SMEM] + [VMEM] * 4, [((peers * packed, 128), bf16)],
        source, lowered, angle_tiles.reshape(parts, rows, rows), head, atoms,
        scratch=[pltpu.VMEM((peers * packed, 128), f32)],
    )
    arrived = lax.all_to_all(send.reshape(peers, packed // 2, 2, 128), GRAPH, 0, 0, tiled=True)
    ups = jnp.concatenate([ups, other], axis=0)
    step = 2
    while step < blocks:
        other = lax.ppermute(ups, "basis", [(j, j ^ step) for j in range(blocks)])
        ups = jnp.concatenate([ups, other], axis=0)
        step *= 2
    swapped = lax.ppermute(ups, "core", [(0, 1), (1, 0)])
    summed, ids = call(
        lambda *refs: combine_kernel(parts, peers, *refs), "combine", [VMEM],
        [((peers * blocks, 128), bf16), ((HEAD, 128), f32)],
        arrived.reshape(peers * packed, 128),
        scratch=[pltpu.VMEM((peers * packed, 128), f32)],
    )
    far = blocks * z_size
    columns = lax.all_to_all(summed.reshape(near, far, 128), ("x", "core"), 0, 0, tiled=True)
    columns = jnp.swapaxes(columns, 0, 1)
    columns = lax.all_to_all(columns, ("basis", "z"), 0, 0, tiled=True)
    edge_update, send = call(
        lambda *refs: edge_kernel(peers, *refs), "edges", [SMEM] + [VMEM] * 7,
        [((rows, width), bf16), ((peers, 2 * width // 128, 128), bf16)],
        jnp.stack([core, group]).astype(i32),
        columns.reshape(peers * blocks, 128), ups, swapped, edge_feats,
        res_first, res_second, head, keep=(0,),
        scratch=[pltpu.VMEM((peers * 2 * width // 128, 128), f32)],
    )
    arrived = lax.all_to_all(send, GRAPH, 0, 0, tiled=True)
    (atom_update,) = call(
        atom_kernel, "atoms", [VMEM] * 5, [(atom_feats.shape, bf16)],
        arrived, ids, atom_feats, atom_first, atom_second, keep=(0,),
        scratch=[pltpu.VMEM((peers * 2 * width // 128, 128), f32)],
    )
    return (edge_update, atom_update)


def solution(mesh):
    shape = (mesh.shape["graph"] // 16, 8, 2, mesh.shape["basis"])
    grid = jax.sharding.Mesh(mesh.devices.reshape(shape), GRAPH + ("basis",))
    both = GRAPH + ("basis",)
    in_specs = (
        P(both, None),
        P(),
        P(),
        P(GRAPH, "basis", None, None),
        P(GRAPH),
        P(GRAPH, None),
        P(GRAPH),
        P("basis", None, None),
        P(),
        P(),
        P(both, None),
        P(both, None, None),
        P(both, None),
        P(both, None),
        P(),
        P(),
    )
    out_specs = (P(both, None), P(both, None))
    return jax.shard_map(body, mesh=grid, in_specs=in_specs, out_specs=out_specs, check_vma=False)
```

time: 110 us -> 104 us (0.945)
  starting transfers between devices: 51 us -> 47.7 us
  local copies, waits for them, and re-layouts: 4.26 us -> 1.48 us
  waiting for transfers between devices: 29.3 us -> 26.8 us
  blocking collectives: 15.4 us -> 17.3 us
    all_to_all x2 -> x3, waiting for transfers between devices: 13.4 us -> 17.5 us  [the longest x1 11.5 us: body(): columns = lax.all_to_all(columns, ('basis', 'z'), 0, 0, tiled=True)]
    all_to_all x1, waiting for transfers between devices: 7.1 us -> 3.31 us  [body(): lowered = lax.all_to_all(lowered, 'basis', 0, 0, tiled=True)]
    unnamed x37 -> x28, local copies, waits for them, and re-layouts: 4.24 us -> 0.73 us
    all_to_all x2 -> x3, starting transfers between devices: 31.2 us -> 28 us  [the longest x1 15.7 us: body(): lax.all_to_all(send.reshape(peers, packed // 2, 2, 128), GRAPH, 0, 0, til...]
    ppermute x3 -> x2, waiting for transfers between devices: 7.72 us -> 5.63 us  [body(): other = lax.ppermute(ups, 'basis', [(j, j ^ step) for j in range(blocks)])]
    all_to_all x1, blocking collectives: 15.4 us -> 17.3 us  [body(): arrived = lax.all_to_all(send, GRAPH, 0, 0, tiled=True)]
    ppermute x1 -> x2, starting transfers between devices: 6.34 us -> 5.69 us  [the longest x1 3.35 us: body(): other = lax.ppermute(ups, 'basis', [(j, j ^ 1) for j in range(blocks)])]
    ppermute x3 -> x2, starting transfers between devices: 5.82 us -> 6.41 us  [body(): other = lax.ppermute(ups, 'basis', [(j, j ^ step) for j in range(blocks)])]
  transfers between devices with their start and end apart: 7 -> 8, of which waited for: 6 -> 6; matrix products, arithmetic and copies ran while one was open for 0% -> 1% of each run, Pallas kernels for 1% -> 1%
where the time goes in v3:
time: 104 us; the launch traced here: 103 us
  starting transfers between devices  47.7 us (46%)
  waiting for transfers between devices  26.8 us (26%)
  blocking collectives  17.3 us (17%)
  Pallas kernels  8.88 us (9%)
  local copies, waits for them, and re-layouts  1.48 us (1%)
    all_to_all x1, blocking collectives, body(): arrived = lax.all_to_all(send, GRAPH, 0, 0, tiled=True)  17.3 us
    all_to_all x1, starting transfers between devices, body(): lax.all_to_all(send.reshape(peers, packed // 2, 2, 128), GRAPH, 0, 0, til...  15.7 us
    all_to_all x1, waiting for transfers between devices, body(): columns = lax.all_to_all(columns, ('basis', 'z'), 0, 0, tiled=True)  11.5 us
    pallas_call x6, Pallas kernels, call(): pl.pallas_call(kernel, name=name, in_specs=specs, out_specs=[VMEM] * len(...  8.88 us
    all_to_all x1, starting transfers between devices, body(): columns = lax.all_to_all(columns, ('basis', 'z'), 0, 0, tiled=True)  7.74 us
    all_to_all x1, starting transfers between devices, body(): lowered = lax.all_to_all(lowered, 'basis', 0, 0, tiled=True)  7.64 us
    ppermute x2, starting transfers between devices, body(): other = lax.ppermute(ups, 'basis', [(j, j ^ step) for j in range(blocks)])  6.41 us
    ppermute x2, waiting for transfers between devices, body(): other = lax.ppermute(ups, 'basis', [(j, j ^ step) for j in range(blocks)])  5.63 us
  transfers between devices with their start and end apart: 8, of which 6 were waited for; matrix products, arithmetic and copies ran while one was open for 1% of the time, Pallas kernels for 1%

profile of v3, /device:TPU:1, one launch (start us, length us, event | category | flops | bytes accessed | tf_op | source)
XLA Modules:
  0.0 103.1 jit_solution(18142165071019129648)
XLA Ops:
  0.6 0.0 copy-start
  0.6 0.0 copy-start.1
  0.7 2.4 %lower.1 = bf16[8,64,128]{2,1,0:T(8,128)(2,1)} custom-call(bf16[128,512]{1,0:T(8,128)(2,1)} %refs_4_.1, bf16[512,512]{1,0:T(8,128)(2,1)} %refs_1_.1, bf16[64,512]{1,0:T(8,128)(2,1)} %bitcast.22), custom_call_target="tpu_custom_call" | custom-call | tf_op jit(solution)/shard_map/lower/pallas_call | solution.py:164
  3.0 7.6 %all-to-all-start = ((bf16[8,64,128]{2,1,0:T(8,128)(2,1)}), bf16[8,64,128]{2,1,0:T(8,128)(2,1)S(1)}, u32[]{:S(2)}, u32[]{:S(2)}) async-start(bf16[8,64,128]{2,1,0:T(8,128)(2,1)} %lower.1), calls=%async_computation | async-start | bytes 262144 | tf_op jit(solution)/shard_map/all_to_all | solution.py:213
  10.7 0.0 copy-done
  10.7 0.0 copy-start.13
  10.7 3.4 %collective-permute-start = (bf16[32,512]{1,0:T(8,128)(2,1)S(1)}, bf16[32,512]{1,0:T(8,128)(2,1)S(1)}, u32[]{:S(2)}, u32[]{:S(2)}) collective-permute-start(bf16[32,512]{1,0:T(8,128)(2,1)S(1)} %dynamic-slice_bitcast_fusion), channel_id=1, source_target_pairs={{0,1},{1,0},{2,3},{3,2},{4,5},{5,4},{6,7},{7,6},{8,9},{9,8},{10,11... | collective-permute-start | bytes 98312 | tf_op jit(solution)/shard_map/ppermute | solution.py:214
  14.1 0.0 copy-done.13
  14.1 0.0 copy-start.11
  14.1 0.0 copy-start.12
  14.1 0.0 copy-start.8
  14.1 0.0 copy-start.9
  14.1 0.0 copy-start.10
  14.1 0.6 copy-done.11
  14.7 0.0 copy-done.12
  14.8 0.0 copy-done.8
  14.8 0.0 copy-done.9
  14.8 0.0 copy-done.10
  14.8 0.2 tables.1
  15.0 0.4 collective-permute-done
  15.4 3.3 %all-to-all-done.lowered_ref = bf16[8,64,128]{2,1,0:T(8,128)(2,1)S(1)} async-done(((bf16[8,64,128]{2,1,0:T(8,128)(2,1)}), bf16[8,64,128]{2,1,0:T(8,128)(2,1)S(1)}, u32[]{:S(2)}, u32[]{:S(2)}) %all-to-all-start) | async-done | bytes 131104 | tf_op jit(solution)/shard_map/all_to_all | solution.py:213
  18.7 0.0 copy-done.1
  18.7 2.0 %products.1 = bf16[1664,128]{1,0:T(8,128)(2,1)} custom-call(s32[24]{0:T(128)S(1)} %broadcast_clamp_fusion.source_ref, bf16[8,64,128]{2,1,0:T(8,128)(2,1)S(1)} %all-to-all-done.lowered_ref, bf16[24,128,128]{2,1,0:T(8,128)(2,1)S(1)} %bitcast.16, f32[8,128]{1,0:T(8,128)S(1)} %get-tuple-element.15.head_ref.refs_7_, f32[64,128]{1,0:T(8,128)S(1)} %get-tuple-element.16.atoms_ref), custom_call_target="tpu_custom_call" | custom-call | tf_op jit(solution)/shard_map/products/pallas_call | solution.py:164
  20.7 15.7 %all-to-all-start.1 = ((bf16[64,13,2,128]{3,2,1,0:T(2,128)(2,1)}), bf16[64,13,2,128]{3,2,1,0:T(2,128)(2,1)S(1)}, u32[]{:S(2)}, u32[]{:S(2)}) async-start(bf16[64,13,2,128]{3,2,1,0:T(2,128)(2,1)} %bitcast.9), calls=%async_computation.1 | async-start | bytes 851968 | tf_op jit(solution)/shard_map/all_to_all | solution.py:228
  36.4 1.9 %collective-permute-start.1 = (bf16[64,512]{1,0:T(8,128)(2,1)S(1)}, bf16[64,512]{1,0:T(8,128)(2,1)S(1)}, u32[]{:S(2)}, u32[]{:S(2)}) collective-permute-start(bf16[64,512]{1,0:T(8,128)(2,1)S(1)} %pad_maximum_fusion.2), channel_id=1, source_target_pairs={{0,2},{1,3},{2,0},{3,1},{4,6},{5,7},{6,4},{7,5},{8,10},{9,11},{10,... | collective-permute-start | bytes 196616 | tf_op jit(solution)/shard_map/ppermute | solution.py:232
  38.3 5.6 %collective-permute-done.1 = bf16[64,512]{1,0:T(8,128)(2,1)S(1)} collective-permute-done((bf16[64,512]{1,0:T(8,128)(2,1)S(1)}, bf16[64,512]{1,0:T(8,128)(2,1)S(1)}, u32[]{:S(2)}, u32[]{:S(2)}) %collective-permute-start.1) | collective-permute-done | bytes 65568 | tf_op jit(solution)/shard_map/ppermute | solution.py:232
  44.0 4.5 %collective-permute-start.2 = (bf16[128,512]{1,0:T(8,128)(2,1)S(1)}, bf16[128,512]{1,0:T(8,128)(2,1)S(1)}, u32[]{:S(2)}, u32[]{:S(2)}) collective-permute-start(bf16[128,512]{1,0:T(8,128)(2,1)S(1)} %pad_maximum_fusion.1), channel_id=1, source_target_pairs={{0,4},{1,5},{2,6},{3,7},{4,0},{5,1},{6,2},{7,3},{8,12},{9,13},{10,... | collective-permute-start | bytes 393224 | tf_op jit(solution)/shard_map/ppermute | solution.py:232
  48.5 3.2 %all-to-all-done.1 = bf16[64,13,2,128]{3,2,1,0:T(2,128)(2,1)S(1)} async-done(((bf16[64,13,2,128]{3,2,1,0:T(2,128)(2,1)}), bf16[64,13,2,128]{3,2,1,0:T(2,128)(2,1)S(1)}, u32[]{:S(2)}, u32[]{:S(2)}) %all-to-all-start.1) | async-done | bytes 426016 | tf_op jit(solution)/shard_map/all_to_all | solution.py:228
  51.7 1.3 %combine.1 = (bf16[512,128]{1,0:T(8,128)(2,1)}, f32[8,128]{1,0:T(8,128)S(1)}) custom-call(bf16[1664,128]{1,0:T(8,128)(2,1)S(1)} %bitcast.15), custom_call_target="tpu_custom_call" | custom-call | tf_op jit(solution)/shard_map/combine/pallas_call | solution.py:164
  53.0 0.0 copy-start.6
  53.0 4.6 %all-to-all-start.2 = ((bf16[8,64,128]{2,1,0:T(8,128)(2,1)}), bf16[8,64,128]{2,1,0:T(8,128)(2,1)S(1)}, u32[]{:S(2)}, u32[]{:S(2)}) async-start(bf16[8,64,128]{2,1,0:T(8,128)(2,1)} %bitcast.11), calls=%async_computation.2 | async-start | bytes 262144 | tf_op jit(solution)/shard_map/all_to_all | solution.py:243
  57.5 0.0 copy-start.4
  57.5 0.0 copy-start.5
  57.5 0.0 collective-permute-done.2
  57.6 2.3 %collective-permute-start.3 = (bf16[256,512]{1,0:T(8,128)(2,1)S(1)}, bf16[256,512]{1,0:T(8,128)(2,1)S(1)}, u32[]{:S(2)}, u32[]{:S(2)}) collective-permute-start(bf16[256,512]{1,0:T(8,128)(2,1)S(1)} %pad_maximum_fusion.refs_2_), channel_id=1, source_target_pairs={{0,8},{8,0},{1,9},{9,1},{2,10},{10,2},{3,11},{11,3},{4,12},{12,4},... | collective-permute-start | bytes 786440 | tf_op jit(solution)/shard_map/ppermute | solution.py:235
  59.9 2.9 %all-to-all-done.2 = bf16[8,64,128]{2,1,0:T(8,128)(2,1)S(1)} async-done(((bf16[8,64,128]{2,1,0:T(8,128)(2,1)}), bf16[8,64,128]{2,1,0:T(8,128)(2,1)S(1)}, u32[]{:S(2)}, u32[]{:S(2)}) %all-to-all-start.2) | async-done | bytes 131104 | tf_op jit(solution)/shard_map/all_to_all | solution.py:243
  62.8 0.7 copy.20
  63.5 7.7 %all-to-all-start.3 = ((bf16[64,8,128]{2,1,0:T(8,128)(2,1)}), bf16[64,8,128]{2,1,0:T(8,128)(2,1)S(1)}, u32[]{:S(2)}, u32[]{:S(2)}) async-start(bf16[64,8,128]{2,1,0:T(8,128)(2,1)} %copy.20), calls=%async_computation.3 | async-start | bytes 262144 | tf_op jit(solution)/shard_map/all_to_all | solution.py:245
  71.3 0.1 pad_add_fusion.refs_0_
  71.3 0.0 collective-permute-done.3.refs_3_
  71.3 11.5 %all-to-all-done.3 = bf16[64,8,128]{2,1,0:T(8,128)(2,1)S(1)} async-done(((bf16[64,8,128]{2,1,0:T(8,128)(2,1)}), bf16[64,8,128]{2,1,0:T(8,128)(2,1)S(1)}, u32[]{:S(2)}, u32[]{:S(2)}) %all-to-all-start.3) | async-done | bytes 131104 | tf_op jit(solution)/shard_map/all_to_all | solution.py:245
  82.8 0.0 copy-done.6
  82.8 0.0 copy-done.4
  82.8 0.0 copy-done.5
  82.8 0.0 copy-start.2
  82.9 0.0 copy-start.3
  82.9 1.9 %edges.1 = (bf16[128,512]{1,0:T(8,128)(2,1)}, bf16[64,8,128]{2,1,0:T(8,128)(2,1)S(1)}) custom-call(s32[2]{0:T(128)S(1)} %pad_add_fusion.refs_0_, bf16[512,128]{1,0:T(8,128)(2,1)S(1)} %bitcast.17, bf16[256,512]{1,0:T(8,128)(2,1)S(1)} %pad_maximum_fusion.refs_2_, bf16[256,512]{1,0:T(8,128)(2,1)S(1)} %collective-permute-done.3.refs_3_, ...), custom_call_target="tpu_custom_call" | custom-call | tf_op jit(solution)/shard_map/edges/pallas_call | solution.py:164
  84.8 0.0 copy-start.7
  84.8 17.3 %all_to_all.25.arrived_ref = bf16[64,8,128]{2,1,0:T(8,128)(2,1)S(1)} all-to-all(bf16[64,8,128]{2,1,0:T(8,128)(2,1)S(1)} %get-tuple-element.20), channel_id=1, replica_groups=mesh['x'=4,'z'=8,'core'=2,'basis'=8] {'x','z','core'}, dimensions={0} | all-to-all | bytes 262144 | tf_op jit(solution)/shard_map/all_to_all | solution.py:254
  102.0 0.0 copy-done.2
  102.0 0.0 copy-done.3
  102.0 0.0 copy-done.7
  102.0 1.1 %atoms.1 = bf16[32,512]{1,0:T(8,128)(2,1)} custom-call(bf16[64,8,128]{2,1,0:T(8,128)(2,1)S(1)} %all_to_all.25.arrived_ref, f32[8,128]{1,0:T(8,128)S(1)} %get-tuple-element.21.ids_ref, bf16[32,512]{1,0:T(8,128)(2,1)S(1)} %copy-done.7, bf16[512,512]{1,0:T(8,128)(2,1)S(1)} %copy-done.2, bf16[512,512]{1,0:T(8,128)(2,1)S(1)} %copy-done.3), custom_call_target="tpu_custom_call" | custom-call | tf_op jit(solution)/shard_map/atoms/pallas_call | solution.py:164
  (5 shorter events, 0.1 us)
Async XLA Ops:
  0.6 10.0 %copy-start = (bf16[1,64,512]{2,1,0:T(8,128)(2,1)S(1)}, bf16[1,64,512]{2,1,0:T(8,128)(2,1)}, u32[]{:S(2)}) copy-start(bf16[1,64,512]{2,1,0:T(8,128)(2,1)} %param.23) | copy-start | bytes 196612
  0.6 18.0 %copy-start.1 = (bf16[24,1,128,128]{3,2,1,0:T(8,128)(2,1)S(1)}, bf16[24,1,128,128]{3,2,1,0:T(8,128)(2,1)}, u32[]{:S(2)}) copy-start(bf16[24,1,128,128]{3,2,1,0:T(8,128)(2,1)} %param.19) | copy-start | bytes 2359300
  3.0 15.7 %all-to-all-start = ((bf16[8,64,128]{2,1,0:T(8,128)(2,1)}), bf16[8,64,128]{2,1,0:T(8,128)(2,1)S(1)}, u32[]{:S(2)}, u32[]{:S(2)}) async-start(bf16[8,64,128]{2,1,0:T(8,128)(2,1)} %lower.1), calls=%async_computation | async-start | bytes 262144 | tf_op jit(solution)/shard_map/all_to_all | solution.py:213
  10.7 3.4 %copy-start.13 = (s32[24]{0:T(128)S(1)}, s32[24]{0:T(128)}, u32[]{:S(2)}) copy-start(s32[24]{0:T(128)} %param.20) | copy-start | bytes 292
  10.7 4.7 %collective-permute-start = (bf16[32,512]{1,0:T(8,128)(2,1)S(1)}, bf16[32,512]{1,0:T(8,128)(2,1)S(1)}, u32[]{:S(2)}, u32[]{:S(2)}) collective-permute-start(bf16[32,512]{1,0:T(8,128)(2,1)S(1)} %dynamic-slice_bitcast_fusion), channel_id=1, source_target_pairs={{0,1},{1,0},{2,3},{3,2},{4,5},{5,4},{6,7},{7,6},{8,9},{9,8},{10,11... | collective-permute-start | bytes 98312 | tf_op jit(solution)/shard_map/ppermute | solution.py:214
  14.1 0.7 copy-start.11
  14.1 0.7 copy-start.12
  14.1 0.7 copy-start.8
  14.1 0.7 copy-start.9
  14.1 0.7 copy-start.10
  20.7 31.0 %all-to-all-start.1 = ((bf16[64,13,2,128]{3,2,1,0:T(2,128)(2,1)}), bf16[64,13,2,128]{3,2,1,0:T(2,128)(2,1)S(1)}, u32[]{:S(2)}, u32[]{:S(2)}) async-start(bf16[64,13,2,128]{3,2,1,0:T(2,128)(2,1)} %bitcast.9), calls=%async_computation.1 | async-start | bytes 851968 | tf_op jit(solution)/shard_map/all_to_all | solution.py:228
  36.4 7.6 %collective-permute-start.1 = (bf16[64,512]{1,0:T(8,128)(2,1)S(1)}, bf16[64,512]{1,0:T(8,128)(2,1)S(1)}, u32[]{:S(2)}, u32[]{:S(2)}) collective-permute-start(bf16[64,512]{1,0:T(8,128)(2,1)S(1)} %pad_maximum_fusion.2), channel_id=1, source_target_pairs={{0,2},{1,3},{2,0},{3,1},{4,6},{5,7},{6,4},{7,5},{8,10},{9,11},{10,... | collective-permute-start | bytes 196616 | tf_op jit(solution)/shard_map/ppermute | solution.py:232
  44.0 13.6 %collective-permute-start.2 = (bf16[128,512]{1,0:T(8,128)(2,1)S(1)}, bf16[128,512]{1,0:T(8,128)(2,1)S(1)}, u32[]{:S(2)}, u32[]{:S(2)}) collective-permute-start(bf16[128,512]{1,0:T(8,128)(2,1)S(1)} %pad_maximum_fusion.1), channel_id=1, source_target_pairs={{0,4},{1,5},{2,6},{3,7},{4,0},{5,1},{6,2},{7,3},{8,12},{9,13},{10,... | collective-permute-start | bytes 393224 | tf_op jit(solution)/shard_map/ppermute | solution.py:232
  53.0 29.9 %copy-start.6 = (bf16[128,512]{1,0:T(8,128)(2,1)S(1)}, bf16[128,512]{1,0:T(8,128)(2,1)}, u32[]{:S(2)}) copy-start(bf16[128,512]{1,0:T(8,128)(2,1)} %refs_4_.1) | copy-start | bytes 393220
  53.0 9.8 %all-to-all-start.2 = ((bf16[8,64,128]{2,1,0:T(8,128)(2,1)}), bf16[8,64,128]{2,1,0:T(8,128)(2,1)S(1)}, u32[]{:S(2)}, u32[]{:S(2)}) async-start(bf16[8,64,128]{2,1,0:T(8,128)(2,1)} %bitcast.11), calls=%async_computation.2 | async-start | bytes 262144 | tf_op jit(solution)/shard_map/all_to_all | solution.py:243
  57.5 25.3 %copy-start.4 = (bf16[512,512]{1,0:T(8,128)(2,1)S(1)}, bf16[512,512]{1,0:T(8,128)(2,1)}, u32[]{:S(2)}) copy-start(bf16[512,512]{1,0:T(8,128)(2,1)} %refs_5_.3) | copy-start | bytes 1572868
  57.5 25.3 %copy-start.5 = (bf16[512,512]{1,0:T(8,128)(2,1)S(1)}, bf16[512,512]{1,0:T(8,128)(2,1)}, u32[]{:S(2)}) copy-start(bf16[512,512]{1,0:T(8,128)(2,1)} %refs_6_.1) | copy-start | bytes 1572868
  57.6 13.8 %collective-permute-start.3 = (bf16[256,512]{1,0:T(8,128)(2,1)S(1)}, bf16[256,512]{1,0:T(8,128)(2,1)S(1)}, u32[]{:S(2)}, u32[]{:S(2)}) collective-permute-start(bf16[256,512]{1,0:T(8,128)(2,1)S(1)} %pad_maximum_fusion.refs_2_), channel_id=1, source_target_pairs={{0,8},{8,0},{1,9},{9,1},{2,10},{10,2},{3,11},{11,3},{4,12},{12,4},... | collective-permute-start | bytes 786440 | tf_op jit(solution)/shard_map/ppermute | solution.py:235
  63.5 19.3 %all-to-all-start.3 = ((bf16[64,8,128]{2,1,0:T(8,128)(2,1)}), bf16[64,8,128]{2,1,0:T(8,128)(2,1)S(1)}, u32[]{:S(2)}, u32[]{:S(2)}) async-start(bf16[64,8,128]{2,1,0:T(8,128)(2,1)} %copy.20), calls=%async_computation.3 | async-start | bytes 262144 | tf_op jit(solution)/shard_map/all_to_all | solution.py:245
  82.8 19.2 %copy-start.2 = (bf16[512,512]{1,0:T(8,128)(2,1)S(1)}, bf16[512,512]{1,0:T(8,128)(2,1)}, u32[]{:S(2)}) copy-start(bf16[512,512]{1,0:T(8,128)(2,1)} %first_ref.1) | copy-start | bytes 1572868
  82.9 19.2 %copy-start.3 = (bf16[512,512]{1,0:T(8,128)(2,1)S(1)}, bf16[512,512]{1,0:T(8,128)(2,1)}, u32[]{:S(2)}) copy-start(bf16[512,512]{1,0:T(8,128)(2,1)} %second_ref.1) | copy-start | bytes 1572868
  84.8 17.3 %copy-start.7 = (bf16[32,512]{1,0:T(8,128)(2,1)S(1)}, bf16[32,512]{1,0:T(8,128)(2,1)}, u32[]{:S(2)}) copy-start(bf16[32,512]{1,0:T(8,128)(2,1)} %feats_ref.1) | copy-start | bytes 98308

commit v4 on v3

--- a/solution.py
+++ b/solution.py
@@ -10,6 +10,8 @@
 VMEM = pl.BlockSpec(memory_space=pltpu.VMEM)
 SMEM = pl.BlockSpec(memory_space=pltpu.SMEM)
 GRAPH = ("x", "z", "core")
+STEPS = (4, 2, 1)
+ORDER = (0, 4, 2, 6)
 HEAD = 8
 OFFSET = 256
 
@@ -26,7 +28,13 @@
     return lax.dot_general(a, b, (((left,), (right,)), ((), ())), preferred_element_type=f32)
 
 
-def lower_kernel(z_size, edge_ref, pre_ref, down_ref, out_ref):
+def lower_kernel(
+    sizes, me_ref, edge_ref, pre_ref, down_ref, source_ref, owner_ref, target_ref, slot_ref, slot_owner_ref,
+    slot_atom_ref, out_ref, head_ref, atoms_ref, sources_ref,
+):
+    z_size = sizes[0]
+    sources_ref[...] = source_ref[...]
+    tables(sizes, me_ref, owner_ref, target_ref, slot_ref, slot_owner_ref, slot_atom_ref, head_ref, atoms_ref)
     projected = silu(dot(edge_ref[...], pre_ref[...], 1, 0)).astype(bf16)
     lowered = silu(dot(down_ref[...], projected, 1, 1)).astype(bf16)
     narrow = lowered.shape[0]
@@ -43,7 +51,7 @@
     return jnp.sum(jnp.where(iota((n, n), 0) == iota((n, n), 1), row, 0), axis=1, keepdims=True)
 
 
-def table_kernel(sizes, me_ref, owner_ref, target_ref, slot_ref, slot_owner_ref, slot_atom_ref, head_ref, atoms_ref):
+def tables(sizes, me_ref, owner_ref, target_ref, slot_ref, slot_owner_ref, slot_atom_ref, head_ref, atoms_ref):
     me = me_ref[0]
     parts = owner_ref.shape[1]
     slots = slot_owner_ref.shape[1]
@@ -81,7 +89,7 @@
     peers = atoms_ref.shape[0]
     rows = parts + 2
     for p in range(parts):
-        product = dot(lowered_ref[source_ref[p]], tiles_ref[p], 1, 1)
+        product = dot(lowered_ref[source_ref[0, p]], tiles_ref[p], 1, 1)
         scratch[pl.ds(p, peers, stride=rows), :] = product
     scratch[pl.ds(parts, peers, stride=rows), :] = jnp.broadcast_to(head_ref[0:1, :], (peers, 128))
     scratch[pl.ds(parts + 1, peers, stride=rows), :] = atoms_ref[...]
@@ -112,18 +120,16 @@
 
 
 def edge_kernel(
-    peers, at_ref, columns_ref, up_ref, swapped_ref, edge_ref, first_ref, second_ref, head_ref, out_ref, send_ref, scratch
+    at_ref, columns_ref, up_ref, other_ref, edge_ref, first_ref, second_ref, head_ref, out_ref, send_ref, scratch
 ):
-    core, group = at_ref[0], at_ref[1]
-    blocks = columns_ref.shape[0] // peers
-    half = up_ref.shape[0] // blocks
+    narrow = up_ref.shape[0] // len(ORDER)
     triplet = jnp.zeros(out_ref.shape, f32)
-    for side, ref in ((core, up_ref), (1 - core, swapped_ref)):
-        found = [
-            columns_ref[pl.ds(pl.multiple_of(((group ^ j) * 2 + side) * half, half), half), :]
-            for j in range(blocks)
-        ]
-        triplet = triplet + dot(jnp.concatenate(found, axis=0).astype(bf16), ref[...], 0, 0)
+    for flip, ref in ((0, up_ref), (STEPS[-1], other_ref)):
+        found = []
+        for d in ORDER:
+            start = pl.multiple_of((at_ref[0] ^ (flip ^ d)) * narrow, narrow)
+            found.append(columns_ref[pl.ds(start, narrow), :])
+        triplet = triplet + dot(jnp.concatenate(found, axis=0), ref[...], 0, 0)
     joined = (edge_ref[...].astype(f32) + triplet).astype(bf16)
     inner = silu(dot(joined, first_ref[...], 1, 0)).astype(bf16)
     second = silu(dot(inner, second_ref[...], 1, 0))
@@ -156,14 +162,13 @@
     out_ref[...] = (feats_ref[...].astype(f32) + dot(hidden, second_ref[...], 1, 0)).astype(bf16)
 
 
-def call(kernel, name, specs, outs, *args, scratch=(), keep=(), space=pltpu.VMEM):
+def call(kernel, specs, outs, *args, scratch=(), keep=(), space=pltpu.VMEM):
     args = [
         pltpu.with_memory_space_constraint(a, space) if s is VMEM else a
         for a, s in zip(args, specs)
     ]
     return pl.pallas_call(
         kernel,
-        name=name,
         in_specs=specs,
         out_specs=[VMEM] * len(outs),
         out_shape=[
@@ -173,6 +178,11 @@
         scratch_shapes=scratch,
         compiler_params=pltpu.CompilerParams(vmem_limit_bytes=16 << 20),
     )(*args)
+
+
+def shifted(x, i):
+    order = [(j, j ^ STEPS[i]) for j in range(2 * STEPS[0])]
+    return lax.ppermute(x, "basis", order)
 
 
 def body(
@@ -201,40 +211,30 @@
     packed = parts + 2
     near = peers // z_size
     me = lax.axis_index(GRAPH).astype(i32).reshape(1)
-    core, group = lax.axis_index("core"), lax.axis_index("basis")
-    half = narrow // 2
-
-    (lowered,) = call(
-        lambda *refs: lower_kernel(z_size, *refs), "lower", [VMEM] * 3, [((blocks, narrow, rows), bf16)],
-        edge_feats, pre_weight, down_weight.T, space=pltpu.HBM,
-    )
-    lowered, ups = lax.optimization_barrier((lowered, up_weight))
-    ups = lax.dynamic_slice_in_dim(ups[0], core * half, half, 0)
+    group = lax.axis_index("basis")
+
+    lowered, head, atoms, source = call(
+        lambda *refs: lower_kernel((z_size, blocks), *refs), [SMEM] + [VMEM] * 9,
+        [((blocks, narrow, rows), bf16), ((HEAD, 128), f32), ((peers, 128), f32), ((1, parts), i32)],
+        me, edge_feats, pre_weight, down_weight.T, part_source.reshape(1, parts), part_owner.reshape(1, parts),
+        part_target.reshape(1, parts), edge_slot, slot_owner.reshape(1, -1), slot_atom, space=pltpu.HBM,
+    )
+    lowered, ups = lax.optimization_barrier((lowered, up_weight[0]))
     lowered = lax.all_to_all(lowered, "basis", 0, 0, tiled=True)
-    other = lax.ppermute(ups, "basis", [(j, j ^ 1) for j in range(blocks)])
-    lowered, other = lax.optimization_barrier((lowered, other))
-    head, atoms = call(
-        lambda *refs: table_kernel((z_size, blocks), *refs), "tables", [SMEM] + [VMEM] * 5,
-        [((HEAD, 128), f32), ((peers, 128), f32)],
-        me, part_owner.reshape(1, parts), part_target.reshape(1, parts), edge_slot,
-        slot_owner.reshape(1, -1), slot_atom,
-    )
-    source = jnp.clip(part_source, 0, blocks - 1)
+    other = shifted(ups, 0)
+    at = group.astype(i32).reshape(1)
     (send,) = call(
-        product_kernel, "products", [SMEM] + [VMEM] * 4, [((peers * packed, 128), bf16)],
+        product_kernel, [SMEM] + [VMEM] * 4, [((peers * packed, 128), bf16)],
         source, lowered, angle_tiles.reshape(parts, rows, rows), head, atoms,
         scratch=[pltpu.VMEM((peers * packed, 128), f32)],
     )
     arrived = lax.all_to_all(send.reshape(peers, packed // 2, 2, 128), GRAPH, 0, 0, tiled=True)
     ups = jnp.concatenate([ups, other], axis=0)
-    step = 2
-    while step < blocks:
-        other = lax.ppermute(ups, "basis", [(j, j ^ step) for j in range(blocks)])
-        ups = jnp.concatenate([ups, other], axis=0)
-        step *= 2
-    swapped = lax.ppermute(ups, "core", [(0, 1), (1, 0)])
+    ups = jnp.concatenate([ups, shifted(ups, 1)], axis=0)
+    other = shifted(ups, 2)
+    arrived, at = lax.optimization_barrier((arrived, at))
     summed, ids = call(
-        lambda *refs: combine_kernel(parts, peers, *refs), "combine", [VMEM],
+        lambda *refs: combine_kernel(parts, peers, *refs), [VMEM],
         [((peers * blocks, 128), bf16), ((HEAD, 128), f32)],
         arrived.reshape(peers * packed, 128),
         scratch=[pltpu.VMEM((peers * packed, 128), f32)],
@@ -242,18 +242,18 @@
     far = blocks * z_size
     columns = lax.all_to_all(summed.reshape(near, far, 128), ("x", "core"), 0, 0, tiled=True)
     columns = jnp.swapaxes(columns, 0, 1)
+    columns, other = lax.optimization_barrier((columns, other))
     columns = lax.all_to_all(columns, ("basis", "z"), 0, 0, tiled=True)
     edge_update, send = call(
-        lambda *refs: edge_kernel(peers, *refs), "edges", [SMEM] + [VMEM] * 7,
+        edge_kernel, [SMEM] + [VMEM] * 7,
         [((rows, width), bf16), ((peers, 2 * width // 128, 128), bf16)],
-        jnp.stack([core, group]).astype(i32),
-        columns.reshape(peers * blocks, 128), ups, swapped, edge_feats,
+        at, columns.reshape(peers * blocks, 128), ups, other, edge_feats,
         res_first, res_second, head, keep=(0,),
         scratch=[pltpu.VMEM((peers * 2 * width // 128, 128), f32)],
     )
     arrived = lax.all_to_all(send, GRAPH, 0, 0, tiled=True)
     (atom_update,) = call(
-        atom_kernel, "atoms", [VMEM] * 5, [(atom_feats.shape, bf16)],
+        atom_kernel, [VMEM] * 5, [(atom_feats.shape, bf16)],
         arrived, ids, atom_feats, atom_first, atom_second, keep=(0,),
         scratch=[pltpu.VMEM((peers * 2 * width // 128, 128), f32)],
     )

time: 104 us -> 109 us (1.048)
  blocking collectives: 17.3 us -> 51.5 us
  starting transfers between devices: 47.7 us -> 27.7 us
  waiting for transfers between devices: 26.8 us -> 20.4 us
  Pallas kernels: 8.88 us -> 7.5 us
  local copies, waits for them, and re-layouts: 1.48 us -> 0.16 us
    all_to_all x0 -> x2, blocking collectives: none -> 35.6 us  [the longest x1 20.2 us: body(): columns = lax.all_to_all(columns, ('basis', 'z'), 0, 0, tiled=True)]
    all_to_all x2 -> x0, starting transfers between devices: 15.4 us -> none  [the longest x1 7.74 us: body(): columns = lax.all_to_all(columns, ('basis', 'z'), 0, 0, tiled=True)]
    all_to_all x2 -> x0, waiting for transfers between devices: 14.8 us -> none  [the longest x1 11.5 us: body(): columns = lax.all_to_all(columns, ('basis', 'z'), 0, 0, tiled=True)]
    ppermute x4 -> x3, waiting for transfers between devices: 5.98 us -> 15.1 us  [shifted(): return lax.ppermute(x, 'basis', order)]
    ppermute x4 -> x3, starting transfers between devices: 12.1 us -> 6 us  [shifted(): return lax.ppermute(x, 'basis', order)]
    all_to_all x1, waiting for transfers between devices: 3.19 us -> 0.01 us  [body(): lax.all_to_all(send.reshape(peers, packed // 2, 2, 128), GRAPH, 0, 0, til...]
    all_to_all x1, waiting for transfers between devices: 2.86 us -> 5.24 us  [body(): lax.all_to_all(summed.reshape(near, far, 128), ('x', 'core'), 0, 0, tiled...]
    all_to_all x1, starting transfers between devices: 4.56 us -> 6.06 us  [body(): lax.all_to_all(summed.reshape(near, far, 128), ('x', 'core'), 0, 0, tiled...]
  transfers between devices with their start and end apart: 8 -> 5, of which waited for: 6 -> 3; matrix products, arithmetic and copies ran while one was open for 1% -> 0% of each run, Pallas kernels for 1% -> 1%
where the time goes in v4:
time: 109 us; the launch traced here: 108 us
  blocking collectives  51.5 us (47%)
  starting transfers between devices  27.7 us (25%)
  waiting for transfers between devices  20.4 us (19%)
  Pallas kernels  7.5 us (7%)
    all_to_all x1, blocking collectives, body(): columns = lax.all_to_all(columns, ('basis', 'z'), 0, 0, tiled=True)  20.2 us
    all_to_all x1, blocking collectives, body(): arrived = lax.all_to_all(send, GRAPH, 0, 0, tiled=True)  16 us
    all_to_all x1, starting transfers between devices, body(): lax.all_to_all(send.reshape(peers, packed // 2, 2, 128), GRAPH, 0, 0, til...  15.6 us
    all_to_all x1, blocking collectives, body(): lowered = lax.all_to_all(lowered, 'basis', 0, 0, tiled=True)  15.4 us
    ppermute x3, waiting for transfers between devices, shifted(): return lax.ppermute(x, 'basis', order)  15.1 us
    pallas_call x5, Pallas kernels, call(): pl.pallas_call(kernel, in_specs=specs, out_specs=[VMEM] * len(outs), out_...  7.5 us
    all_to_all x1, starting transfers between devices, body(): lax.all_to_all(summed.reshape(near, far, 128), ('x', 'core'), 0, 0, tiled...  6.06 us
    ppermute x3, starting transfers between devices, shifted(): return lax.ppermute(x, 'basis', order)  6 us
  transfers between devices with their start and end apart: 5, of which 3 were waited for; matrix products, arithmetic and copies ran while one was open for 0% of the time, Pallas kernels for 1%

profile of v4, /device:TPU:1, one launch (start us, length us, event | category | flops | bytes accessed | tf_op | source)
XLA Modules:
  0.0 108.0 jit_solution(8528599877891812822)
XLA Ops:
  0.6 0.0 copy-start
  0.7 1.8 %shard_map.167 = (bf16[8,64,128]{2,1,0:T(8,128)(2,1)S(1)}, f32[8,128]{1,0:T(8,128)S(1)}, f32[64,128]{1,0:T(8,128)S(1)}, s32[1,24]{1,0:T(1,128)S(1)}) custom-call(s32[1]{0:T(128)} %bitcast.refs_0_, bf16[128,512]{1,0:T(8,128)(2,1)} %edge_ref.1, bf16[512,512]{1,0:T(8,128)(2,1)} %refs_2_.1, bf16[64,512]{1,0:T(8,128)(2,1)} %bitcast.21, s32[1,24]{1,0:T(1,128)} %bitcast.22, ...), custom_call_target="tpu_custom_call" | custom-call | tf_op jit(solution)/shard_map/pallas_call | solution.py:170
  2.4 15.4 %all_to_all.25.lowered_ref = bf16[8,64,128]{2,1,0:T(8,128)(2,1)S(1)} all-to-all(bf16[8,64,128]{2,1,0:T(8,128)(2,1)S(1)} %get-tuple-element.18), channel_id=1, replica_groups=mesh['x'=4,'z'=8,'core'=2,'basis'=8] {'basis'}, dimensions={0} | all-to-all | bytes 262144 | tf_op jit(solution)/shard_map/all_to_all | solution.py:223
  17.8 0.0 copy-done
  17.8 2.0 %shard_map.168 = bf16[1664,128]{1,0:T(8,128)(2,1)} custom-call(s32[1,24]{1,0:T(1,128)S(1)} %get-tuple-element.16.source_ref, bf16[8,64,128]{2,1,0:T(8,128)(2,1)S(1)} %all_to_all.25.lowered_ref, bf16[24,128,128]{2,1,0:T(8,128)(2,1)S(1)} %bitcast.15, f32[8,128]{1,0:T(8,128)S(1)} %get-tuple-element.19.head_ref, f32[64,128]{1,0:T(8,128)S(1)} %get-tuple-element.20.atoms_ref), custom_call_target="tpu_custom_call" | custom-call | tf_op jit(solution)/shard_map/pallas_call | solution.py:170
  19.7 0.0 copy-start.7
  19.7 15.6 %all-to-all-start.1 = ((bf16[64,13,2,128]{3,2,1,0:T(2,128)(2,1)}), bf16[64,13,2,128]{3,2,1,0:T(2,128)(2,1)S(1)}, u32[]{:S(2)}, u32[]{:S(2)}) async-start(bf16[64,13,2,128]{3,2,1,0:T(2,128)(2,1)} %bitcast.8), calls=%async_computation.1 | async-start | bytes 851968 | tf_op jit(solution)/shard_map/all_to_all | solution.py:231
  35.3 0.0 copy-done.7
  35.4 2.2 %collective-permute-start = (bf16[64,512]{1,0:T(8,128)(2,1)S(1)}, bf16[64,512]{1,0:T(8,128)(2,1)S(1)}, u32[]{:S(2)}, u32[]{:S(2)}) collective-permute-start(bf16[64,512]{1,0:T(8,128)(2,1)S(1)} %bitcast.18), channel_id=1, source_target_pairs={{0,4},{1,5},{2,6},{3,7},{4,0},{5,1},{6,2},{7,3},{8,12},{9,13},{10,... | collective-permute-start | bytes 196616 | tf_op jit(solution)/shard_map/ppermute | solution.py:185
  37.5 7.1 %collective-permute-done = bf16[64,512]{1,0:T(8,128)(2,1)S(1)} collective-permute-done((bf16[64,512]{1,0:T(8,128)(2,1)S(1)}, bf16[64,512]{1,0:T(8,128)(2,1)S(1)}, u32[]{:S(2)}, u32[]{:S(2)}) %collective-permute-start) | collective-permute-done | bytes 65568 | tf_op jit(solution)/shard_map/ppermute | solution.py:185
  44.7 1.9 %collective-permute-start.1 = (bf16[128,512]{1,0:T(8,128)(2,1)S(1)}, bf16[128,512]{1,0:T(8,128)(2,1)S(1)}, u32[]{:S(2)}, u32[]{:S(2)}) collective-permute-start(bf16[128,512]{1,0:T(8,128)(2,1)S(1)} %pad_maximum_fusion), channel_id=1, source_target_pairs={{0,2},{1,3},{2,0},{3,1},{4,6},{5,7},{6,4},{7,5},{8,10},{9,11},{10,... | collective-permute-start | bytes 393224 | tf_op jit(solution)/shard_map/ppermute | solution.py:185
  46.6 8.0 %collective-permute-done.1 = bf16[128,512]{1,0:T(8,128)(2,1)S(1)} collective-permute-done((bf16[128,512]{1,0:T(8,128)(2,1)S(1)}, bf16[128,512]{1,0:T(8,128)(2,1)S(1)}, u32[]{:S(2)}, u32[]{:S(2)}) %collective-permute-start.1) | collective-permute-done | bytes 131104 | tf_op jit(solution)/shard_map/ppermute | solution.py:185
  54.7 1.9 %collective-permute-start.2 = (bf16[256,512]{1,0:T(8,128)(2,1)S(1)}, bf16[256,512]{1,0:T(8,128)(2,1)S(1)}, u32[]{:S(2)}, u32[]{:S(2)}) collective-permute-start(bf16[256,512]{1,0:T(8,128)(2,1)S(1)} %constant_dynamic-update-slice_fusion.up_ref), channel_id=1, source_target_pairs={{0,1},{1,0},{2,3},{3,2},{4,5},{5,4},{6,7},{7,6},{8,9},{9,8},{10,11... | collective-permute-start | bytes 786440 | tf_op jit(solution)/shard_map/ppermute | solution.py:185
  56.6 0.0 all-to-all-done.1
  56.6 0.0 copy-start.3
  56.6 0.0 copy-start.4
  56.6 1.3 %shard_map.169 = (bf16[512,128]{1,0:T(8,128)(2,1)}, f32[8,128]{1,0:T(8,128)S(1)}) custom-call(bf16[1664,128]{1,0:T(8,128)(2,1)S(1)} %bitcast.14), custom_call_target="tpu_custom_call" | custom-call | tf_op jit(solution)/shard_map/pallas_call | solution.py:170
  57.9 6.1 %all-to-all-start.2 = ((bf16[8,64,128]{2,1,0:T(8,128)(2,1)}), bf16[8,64,128]{2,1,0:T(8,128)(2,1)S(1)}, u32[]{:S(2)}, u32[]{:S(2)}) async-start(bf16[8,64,128]{2,1,0:T(8,128)(2,1)} %bitcast.11), calls=%async_computation.2 | async-start | bytes 262144 | tf_op jit(solution)/shard_map/all_to_all | solution.py:243
  64.0 0.0 collective-permute-done.2.other_ref
  64.0 5.2 %all-to-all-done.2 = bf16[8,64,128]{2,1,0:T(8,128)(2,1)S(1)} async-done(((bf16[8,64,128]{2,1,0:T(8,128)(2,1)}), bf16[8,64,128]{2,1,0:T(8,128)(2,1)S(1)}, u32[]{:S(2)}, u32[]{:S(2)}) %all-to-all-start.2) | async-done | bytes 131104 | tf_op jit(solution)/shard_map/all_to_all | solution.py:243
  69.2 0.1 copy.20
  69.3 0.0 copy-start.5
  69.3 20.2 %all_to_all.26 = bf16[64,8,128]{2,1,0:T(8,128)(2,1)S(1)} all-to-all(bf16[64,8,128]{2,1,0:T(8,128)(2,1)S(1)} %copy.20), channel_id=1, replica_groups=mesh['x'=4,'z'=8,'core'=2,'basis'=8] {'basis','z'}, dimensions={0} | all-to-all | bytes 262144 | tf_op jit(solution)/shard_map/all_to_all | solution.py:246
  89.5 0.0 copy-done.3
  89.5 0.0 copy-done.4
  89.5 0.0 copy-done.5
  89.5 0.0 copy-start.1
  89.6 0.0 copy-start.2
  89.6 1.4 %shard_map.170 = (bf16[128,512]{1,0:T(8,128)(2,1)}, bf16[64,8,128]{2,1,0:T(8,128)(2,1)S(1)}) custom-call(s32[1]{0:T(128)} %bitcast.9.at_ref, bf16[512,128]{1,0:T(8,128)(2,1)S(1)} %bitcast.16, bf16[256,512]{1,0:T(8,128)(2,1)S(1)} %constant_dynamic-update-slice_fusion.up_ref, bf16[256,512]{1,0:T(8,128)(2,1)S(1)} %collective-permute-done.2.other_ref, ...), custom_call_target="tpu_custom_call" | custom-call | tf_op jit(solution)/shard_map/pallas_call | solution.py:170
  90.9 0.0 copy-start.6
  90.9 16.0 %all_to_all.27.arrived_ref = bf16[64,8,128]{2,1,0:T(8,128)(2,1)S(1)} all-to-all(bf16[64,8,128]{2,1,0:T(8,128)(2,1)S(1)} %get-tuple-element.28), channel_id=1, replica_groups=mesh['x'=4,'z'=8,'core'=2,'basis'=8] {'x','z','core'}, dimensions={0} | all-to-all | bytes 262144 | tf_op jit(solution)/shard_map/all_to_all | solution.py:254
  106.9 0.0 copy-done.1
  106.9 0.0 copy-done.2
  106.9 0.0 copy-done.6
  106.9 1.1 %shard_map.171 = bf16[32,512]{1,0:T(8,128)(2,1)} custom-call(bf16[64,8,128]{2,1,0:T(8,128)(2,1)S(1)} %all_to_all.27.arrived_ref, f32[8,128]{1,0:T(8,128)S(1)} %get-tuple-element.29.ids_ref, bf16[32,512]{1,0:T(8,128)(2,1)S(1)} %copy-done.6, bf16[512,512]{1,0:T(8,128)(2,1)S(1)} %copy-done.1, bf16[512,512]{1,0:T(8,128)(2,1)S(1)} %copy-done.2), custom_call_target="tpu_custom_call" | custom-call | tf_op jit(solution)/shard_map/pallas_call | solution.py:170
  (4 shorter events, 0.0 us)
Async XLA Ops:
  0.6 17.1 %copy-start = (bf16[24,1,128,128]{3,2,1,0:T(8,128)(2,1)S(1)}, bf16[24,1,128,128]{3,2,1,0:T(8,128)(2,1)}, u32[]{:S(2)}) copy-start(bf16[24,1,128,128]{3,2,1,0:T(8,128)(2,1)} %param.19) | copy-start | bytes 2359300
  19.7 15.6 %copy-start.7 = (bf16[1,64,512]{2,1,0:T(8,128)(2,1)S(1)}, bf16[1,64,512]{2,1,0:T(8,128)(2,1)}, u32[]{:S(2)}) copy-start(bf16[1,64,512]{2,1,0:T(8,128)(2,1)} %param.23) | copy-start | bytes 196612
  19.7 36.8 %all-to-all-start.1 = ((bf16[64,13,2,128]{3,2,1,0:T(2,128)(2,1)}), bf16[64,13,2,128]{3,2,1,0:T(2,128)(2,1)S(1)}, u32[]{:S(2)}, u32[]{:S(2)}) async-start(bf16[64,13,2,128]{3,2,1,0:T(2,128)(2,1)} %bitcast.8), calls=%async_computation.1 | async-start | bytes 851968 | tf_op jit(solution)/shard_map/all_to_all | solution.py:231
  35.4 9.3 %collective-permute-start = (bf16[64,512]{1,0:T(8,128)(2,1)S(1)}, bf16[64,512]{1,0:T(8,128)(2,1)S(1)}, u32[]{:S(2)}, u32[]{:S(2)}) collective-permute-start(bf16[64,512]{1,0:T(8,128)(2,1)S(1)} %bitcast.18), channel_id=1, source_target_pairs={{0,4},{1,5},{2,6},{3,7},{4,0},{5,1},{6,2},{7,3},{8,12},{9,13},{10,... | collective-permute-start | bytes 196616 | tf_op jit(solution)/shard_map/ppermute | solution.py:185
  44.7 10.0 %collective-permute-start.1 = (bf16[128,512]{1,0:T(8,128)(2,1)S(1)}, bf16[128,512]{1,0:T(8,128)(2,1)S(1)}, u32[]{:S(2)}, u32[]{:S(2)}) collective-permute-start(bf16[128,512]{1,0:T(8,128)(2,1)S(1)} %pad_maximum_fusion), channel_id=1, source_target_pairs={{0,2},{1,3},{2,0},{3,1},{4,6},{5,7},{6,4},{7,5},{8,10},{9,11},{10,... | collective-permute-start | bytes 393224 | tf_op jit(solution)/shard_map/ppermute | solution.py:185
  54.7 9.3 %collective-permute-start.2 = (bf16[256,512]{1,0:T(8,128)(2,1)S(1)}, bf16[256,512]{1,0:T(8,128)(2,1)S(1)}, u32[]{:S(2)}, u32[]{:S(2)}) collective-permute-start(bf16[256,512]{1,0:T(8,128)(2,1)S(1)} %constant_dynamic-update-slice_fusion.up_ref), channel_id=1, source_target_pairs={{0,1},{1,0},{2,3},{3,2},{4,5},{5,4},{6,7},{7,6},{8,9},{9,8},{10,11... | collective-permute-start | bytes 786440 | tf_op jit(solution)/shard_map/ppermute | solution.py:185
  56.6 32.9 %copy-start.3 = (bf16[512,512]{1,0:T(8,128)(2,1)S(1)}, bf16[512,512]{1,0:T(8,128)(2,1)}, u32[]{:S(2)}) copy-start(bf16[512,512]{1,0:T(8,128)(2,1)} %first_ref.2) | copy-start | bytes 1572868
  56.6 32.9 %copy-start.4 = (bf16[512,512]{1,0:T(8,128)(2,1)S(1)}, bf16[512,512]{1,0:T(8,128)(2,1)}, u32[]{:S(2)}) copy-start(bf16[512,512]{1,0:T(8,128)(2,1)} %second_ref.2) | copy-start | bytes 1572868
  57.9 11.3 %all-to-all-start.2 = ((bf16[8,64,128]{2,1,0:T(8,128)(2,1)}), bf16[8,64,128]{2,1,0:T(8,128)(2,1)S(1)}, u32[]{:S(2)}, u32[]{:S(2)}) async-start(bf16[8,64,128]{2,1,0:T(8,128)(2,1)} %bitcast.11), calls=%async_computation.2 | async-start | bytes 262144 | tf_op jit(solution)/shard_map/all_to_all | solution.py:243
  69.3 20.2 %copy-start.5 = (bf16[128,512]{1,0:T(8,128)(2,1)S(1)}, bf16[128,512]{1,0:T(8,128)(2,1)}, u32[]{:S(2)}) copy-start(bf16[128,512]{1,0:T(8,128)(2,1)} %edge_ref.1) | copy-start | bytes 393220
  89.5 17.4 %copy-start.1 = (bf16[512,512]{1,0:T(8,128)(2,1)S(1)}, bf16[512,512]{1,0:T(8,128)(2,1)}, u32[]{:S(2)}) copy-start(bf16[512,512]{1,0:T(8,128)(2,1)} %first_ref.3) | copy-start | bytes 1572868
  89.6 17.4 %copy-start.2 = (bf16[512,512]{1,0:T(8,128)(2,1)S(1)}, bf16[512,512]{1,0:T(8,128)(2,1)}, u32[]{:S(2)}) copy-start(bf16[512,512]{1,0:T(8,128)(2,1)} %second_ref.3) | copy-start | bytes 1572868
  90.9 16.0 %copy-start.6 = (bf16[32,512]{1,0:T(8,128)(2,1)S(1)}, bf16[32,512]{1,0:T(8,128)(2,1)}, u32[]{:S(2)}) copy-start(bf16[32,512]{1,0:T(8,128)(2,1)} %feats_ref.1) | copy-start | bytes 98308

commit v5 on v4

--- a/solution.py
+++ b/solution.py
@@ -29,19 +29,15 @@
 
 
 def lower_kernel(
-    sizes, me_ref, edge_ref, pre_ref, down_ref, source_ref, owner_ref, target_ref, slot_ref, slot_owner_ref,
-    slot_atom_ref, out_ref, head_ref, atoms_ref, sources_ref,
+    sizes, edge_ref, pre_ref, down_ref, source_ref, owner_ref, target_ref, slot_ref, slot_owner_ref,
+    slot_atom_ref, out_ref, head_ref, atoms_ref, sources_ref, edges_ref,
 ):
-    z_size = sizes[0]
-    sources_ref[...] = source_ref[...]
-    tables(sizes, me_ref, owner_ref, target_ref, slot_ref, slot_owner_ref, slot_atom_ref, head_ref, atoms_ref)
+    edges_ref[...] = edge_ref[...]
+    for p in range(source_ref.shape[1]):
+        sources_ref[0, p] = source_ref[0, p]
+    tables(sizes, owner_ref, target_ref, slot_ref, slot_owner_ref, slot_atom_ref, head_ref, atoms_ref)
     projected = silu(dot(edge_ref[...], pre_ref[...], 1, 0)).astype(bf16)
     lowered = silu(dot(down_ref[...], projected, 1, 1)).astype(bf16)
-    narrow = lowered.shape[0]
-    to, at = iota((narrow, narrow), 0), iota((narrow, narrow), 1)
-    feature = (to // 2 % z_size) * (narrow // z_size) + to // (2 * z_size) * 2 + to % 2
-    order = jnp.where(at == feature, 1.0, 0.0).astype(bf16)
-    lowered = dot(order, lowered, 1, 0).astype(bf16)
     for i in range(out_ref.shape[0]):
         out_ref[i] = lowered
 
@@ -51,15 +47,14 @@
     return jnp.sum(jnp.where(iota((n, n), 0) == iota((n, n), 1), row, 0), axis=1, keepdims=True)
 
 
-def tables(sizes, me_ref, owner_ref, target_ref, slot_ref, slot_owner_ref, slot_atom_ref, head_ref, atoms_ref):
-    me = me_ref[0]
+def tables(sizes, owner_ref, target_ref, slot_ref, slot_owner_ref, slot_atom_ref, head_ref, atoms_ref):
+    me = (lax.axis_index("x") * sizes[0] + lax.axis_index("z")) * 2 + lax.axis_index("core")
     parts = owner_ref.shape[1]
     slots = slot_owner_ref.shape[1]
     rows = slot_ref.shape[1]
     owner = column(owner_ref[...])
     z_size, blocks = sizes
-    x, z, core = owner // (2 * z_size), (owner // 2) % z_size, owner % 2
-    ids = ((x * 2 + core) * blocks + column(target_ref[...])) * z_size + z - OFFSET
+    ids = column(target_ref[...]) * (blocks * z_size) + owner - OFFSET
     place = iota((parts, 128), 1) == (iota((parts, 128), 0) + me * (parts + 2)) % 128
     id_row = jnp.sum(jnp.where(place, ids, 0), axis=0, keepdims=True)
     own_row = slot_owner_ref[...]
@@ -116,18 +111,19 @@
             hits.append(jnp.where(row == ids, 1.0, 0.0).astype(bf16))
         items = arrived_ref[r * 128 : (r + len(hits)) * 128, :]
         total = total + dot(jnp.concatenate(hits, axis=1), items, 1, 0)
-    out_ref[...] = total.astype(bf16)
+    out_ref[...] = total
 
 
 def edge_kernel(
-    at_ref, columns_ref, up_ref, other_ref, edge_ref, first_ref, second_ref, head_ref, out_ref, send_ref, scratch
+    columns_ref, up_ref, other_ref, edge_ref, first_ref, second_ref, head_ref, out_ref, send_ref, scratch
 ):
+    group = lax.axis_index("basis")
     narrow = up_ref.shape[0] // len(ORDER)
     triplet = jnp.zeros(out_ref.shape, f32)
     for flip, ref in ((0, up_ref), (STEPS[-1], other_ref)):
         found = []
         for d in ORDER:
-            start = pl.multiple_of((at_ref[0] ^ (flip ^ d)) * narrow, narrow)
+            start = pl.multiple_of((group ^ (flip ^ d)) * narrow, narrow)
             found.append(columns_ref[pl.ds(start, narrow), :])
         triplet = triplet + dot(jnp.concatenate(found, axis=0), ref[...], 0, 0)
     joined = (edge_ref[...].astype(f32) + triplet).astype(bf16)
@@ -162,17 +158,19 @@
     out_ref[...] = (feats_ref[...].astype(f32) + dot(hidden, second_ref[...], 1, 0)).astype(bf16)
 
 
-def call(kernel, specs, outs, *args, scratch=(), keep=(), space=pltpu.VMEM):
+def call(kernel, specs, outs, *args, scratch=(), keep=(), scalar=(), space=pltpu.VMEM):
     args = [
-        pltpu.with_memory_space_constraint(a, space) if s is VMEM else a
+        pltpu.with_memory_space_constraint(a, space) if s is VMEM or space is pltpu.HBM else a
         for a, s in zip(args, specs)
     ]
     return pl.pallas_call(
         kernel,
         in_specs=specs,
-        out_specs=[VMEM] * len(outs),
+        out_specs=[SMEM if i in scalar else VMEM for i in range(len(outs))],
         out_shape=[
-            jax.ShapeDtypeStruct(shape, dtype) if i in keep else pltpu.VMEM(shape, dtype)
+            jax.ShapeDtypeStruct(shape, dtype)
+            if i in keep
+            else (pltpu.SMEM if i in scalar else pltpu.VMEM)(shape, dtype)
             for i, (shape, dtype) in enumerate(outs)
         ],
         scratch_shapes=scratch,
@@ -209,45 +207,40 @@
     narrow = down_weight.shape[1]
     rows, width = edge_feats.shape
     packed = parts + 2
-    near = peers // z_size
-    me = lax.axis_index(GRAPH).astype(i32).reshape(1)
-    group = lax.axis_index("basis")
-
-    lowered, head, atoms, source = call(
-        lambda *refs: lower_kernel((z_size, blocks), *refs), [SMEM] + [VMEM] * 9,
-        [((blocks, narrow, rows), bf16), ((HEAD, 128), f32), ((peers, 128), f32), ((1, parts), i32)],
-        me, edge_feats, pre_weight, down_weight.T, part_source.reshape(1, parts), part_owner.reshape(1, parts),
-        part_target.reshape(1, parts), edge_slot, slot_owner.reshape(1, -1), slot_atom, space=pltpu.HBM,
-    )
-    lowered, ups = lax.optimization_barrier((lowered, up_weight[0]))
+
+    lowered, head, atoms, source, edges = call(
+        lambda *refs: lower_kernel((z_size, blocks), *refs), [VMEM] * 3 + [SMEM] + [VMEM] * 5,
+        [((blocks, narrow, rows), bf16), ((HEAD, 128), f32), ((peers, 128), f32), ((1, parts), i32), ((rows, width), bf16)],
+        edge_feats, pre_weight, down_weight.T, part_source.reshape(1, parts), part_owner.reshape(1, parts),
+        part_target.reshape(1, parts), edge_slot, slot_owner.reshape(1, -1), slot_atom, scalar=(3,), space=pltpu.HBM,
+    )
+    lowered, ups, angle_tiles = lax.optimization_barrier((lowered, up_weight[0], angle_tiles))
     lowered = lax.all_to_all(lowered, "basis", 0, 0, tiled=True)
     other = shifted(ups, 0)
-    at = group.astype(i32).reshape(1)
     (send,) = call(
         product_kernel, [SMEM] + [VMEM] * 4, [((peers * packed, 128), bf16)],
-        source, lowered, angle_tiles.reshape(parts, rows, rows), head, atoms,
+        pltpu.with_memory_space_constraint(source, pltpu.SMEM), lowered, angle_tiles.reshape(parts, rows, rows), head, atoms,
         scratch=[pltpu.VMEM((peers * packed, 128), f32)],
     )
     arrived = lax.all_to_all(send.reshape(peers, packed // 2, 2, 128), GRAPH, 0, 0, tiled=True)
     ups = jnp.concatenate([ups, other], axis=0)
     ups = jnp.concatenate([ups, shifted(ups, 1)], axis=0)
     other = shifted(ups, 2)
-    arrived, at = lax.optimization_barrier((arrived, at))
     summed, ids = call(
         lambda *refs: combine_kernel(parts, peers, *refs), [VMEM],
-        [((peers * blocks, 128), bf16), ((HEAD, 128), f32)],
+        [((peers * blocks, 128), f32), ((HEAD, 128), f32)],
         arrived.reshape(peers * packed, 128),
         scratch=[pltpu.VMEM((peers * packed, 128), f32)],
     )
-    far = blocks * z_size
-    columns = lax.all_to_all(summed.reshape(near, far, 128), ("x", "core"), 0, 0, tiled=True)
-    columns = jnp.swapaxes(columns, 0, 1)
+    columns = lax.all_to_all(
+        summed.reshape(peers * blocks, 1, 128), ("basis",) + GRAPH, 0, 0, tiled=True
+    )
+    columns = columns.astype(bf16)
     columns, other = lax.optimization_barrier((columns, other))
-    columns = lax.all_to_all(columns, ("basis", "z"), 0, 0, tiled=True)
     edge_update, send = call(
-        edge_kernel, [SMEM] + [VMEM] * 7,
+        edge_kernel, [VMEM] * 7,
         [((rows, width), bf16), ((peers, 2 * width // 128, 128), bf16)],
-        at, columns.reshape(peers * blocks, 128), ups, other, edge_feats,
+        columns.reshape(peers * blocks, 128), ups, other, edges,
         res_first, res_second, head, keep=(0,),
         scratch=[pltpu.VMEM((peers * 2 * width // 128, 128), f32)],
     )

time: 109 us -> 100 us (0.917)
  blocking collectives: 51.5 us -> 31 us
  starting transfers between devices: 27.7 us -> 35.6 us
  waiting for transfers between devices: 20.4 us -> 25 us
    all_to_all x1 -> x0, blocking collectives: 20.2 us -> none  [body(): columns = lax.all_to_all(columns, ('basis', 'z'), 0, 0, tiled=True)]
    all_to_all x1, waiting for transfers between devices: 5.24 us -> 13.9 us  [body(): lax.all_to_all(summed.reshape(peers * blocks, 1, 128), ('basis',) + GRAPH...]
    ppermute x3, waiting for transfers between devices: 15.1 us -> 7.14 us  [shifted(): return lax.ppermute(x, 'basis', order)]
    all_to_all x1, starting transfers between devices: 6.06 us -> 12.6 us  [body(): lax.all_to_all(summed.reshape(peers * blocks, 1, 128), ('basis',) + GRAPH...]
    all_to_all x1, waiting for transfers between devices: 0.01 us -> 4.01 us  [body(): lax.all_to_all(send.reshape(peers, packed // 2, 2, 128), GRAPH, 0, 0, til...]
    ppermute x3, starting transfers between devices: 6 us -> 7.48 us  [shifted(): return lax.ppermute(x, 'basis', order)]
where the time goes in v5:
time: 100 us; the launch traced here: 99.5 us
  starting transfers between devices  35.6 us (36%)
  blocking collectives  31 us (31%)
  waiting for transfers between devices  25 us (25%)
  Pallas kernels  6.9 us (7%)
    all_to_all x1, blocking collectives, body(): arrived = lax.all_to_all(send, GRAPH, 0, 0, tiled=True)  15.7 us
    all_to_all x1, starting transfers between devices, body(): lax.all_to_all(send.reshape(peers, packed // 2, 2, 128), GRAPH, 0, 0, til...  15.6 us
    all_to_all x1, blocking collectives, body(): lowered = lax.all_to_all(lowered, 'basis', 0, 0, tiled=True)  15.4 us
    all_to_all x1, waiting for transfers between devices, body(): lax.all_to_all(summed.reshape(peers * blocks, 1, 128), ('basis',) + GRAPH...  13.9 us
    all_to_all x1, starting transfers between devices, body(): lax.all_to_all(summed.reshape(peers * blocks, 1, 128), ('basis',) + GRAPH...  12.6 us
    ppermute x3, starting transfers between devices, shifted(): return lax.ppermute(x, 'basis', order)  7.48 us
    ppermute x3, waiting for transfers between devices, shifted(): return lax.ppermute(x, 'basis', order)  7.14 us
    pallas_call x5, Pallas kernels, call(): pl.pallas_call(kernel, in_specs=specs, out_specs=[SMEM if i in scalar els...  6.9 us
  transfers between devices with their start and end apart: 5, of which 3 were waited for; matrix products, arithmetic and copies ran while one was open for 0% of the time, Pallas kernels for 1%

profile of v5, /device:TPU:1, one launch (start us, length us, event | category | flops | bytes accessed | tf_op | source)
XLA Modules:
  0.0 99.5 jit_solution(13802741733618192096)
XLA Ops:
  0.6 0.0 copy-start
  0.6 1.6 %shard_map.167 = (bf16[8,64,128]{2,1,0:T(8,128)(2,1)S(1)}, f32[8,128]{1,0:T(8,128)S(1)}, f32[64,128]{1,0:T(8,128)S(1)}, s32[1,24]{1,0:T(1,128)S(4)}, bf16[128,512]{1,0:T(8,128)(2,1)S(1)}) custom-call(bf16[128,512]{1,0:T(8,128)(2,1)} %refs_0_.1, bf16[512,512]{1,0:T(8,128)(2,1)} %refs_1_.1, bf16[64,512]{1,0:T(8,128)(2,1)} %bitcast.21, s32[1,24]{1,0:T(1,128)} %bitcast.22, ...), custom_call_target="tpu_custom_call" | custom-call | tf_op jit(solution)/shard_map/pallas_call | solution.py:166
  2.3 15.4 %all_to_all.20.lowered_ref = bf16[8,64,128]{2,1,0:T(8,128)(2,1)S(1)} all-to-all(bf16[8,64,128]{2,1,0:T(8,128)(2,1)S(1)} %get-tuple-element.18), channel_id=1, replica_groups=mesh['x'=4,'z'=8,'core'=2,'basis'=8] {'basis'}, dimensions={0} | all-to-all | bytes 262144 | tf_op jit(solution)/shard_map/all_to_all | solution.py:218
  17.6 0.0 copy-done
  17.7 1.4 %shard_map.168 = bf16[1664,128]{1,0:T(8,128)(2,1)} custom-call(s32[1,24]{1,0:T(1,128)S(4)} %get-tuple-element.16.source_ref, bf16[8,64,128]{2,1,0:T(8,128)(2,1)S(1)} %all_to_all.20.lowered_ref, bf16[24,128,128]{2,1,0:T(8,128)(2,1)S(1)} %bitcast.15, f32[8,128]{1,0:T(8,128)S(1)} %get-tuple-element.20.head_ref, f32[64,128]{1,0:T(8,128)S(1)} %get-tuple-element.21.atoms_ref), custom_call_target="tpu_custom_call" | custom-call | tf_op jit(solution)/shard_map/pallas_call | solution.py:166
  19.1 0.0 copy-start.6
  19.1 15.6 %all-to-all-start.1 = ((bf16[64,13,2,128]{3,2,1,0:T(2,128)(2,1)}), bf16[64,13,2,128]{3,2,1,0:T(2,128)(2,1)S(1)}, u32[]{:S(2)}, u32[]{:S(2)}) async-start(bf16[64,13,2,128]{3,2,1,0:T(2,128)(2,1)} %bitcast.7), calls=%async_computation.1 | async-start | bytes 851968 | tf_op jit(solution)/shard_map/all_to_all | solution.py:225
  34.7 0.0 copy-done.6
  34.7 2.2 %collective-permute-start = (bf16[64,512]{1,0:T(8,128)(2,1)S(1)}, bf16[64,512]{1,0:T(8,128)(2,1)S(1)}, u32[]{:S(2)}, u32[]{:S(2)}) collective-permute-start(bf16[64,512]{1,0:T(8,128)(2,1)S(1)} %bitcast.18), channel_id=1, source_target_pairs={{0,4},{1,5},{2,6},{3,7},{4,0},{5,1},{6,2},{7,3},{8,12},{9,13},{10,... | collective-permute-start | bytes 196616 | tf_op jit(solution)/shard_map/ppermute | solution.py:183
  36.9 7.1 %collective-permute-done = bf16[64,512]{1,0:T(8,128)(2,1)S(1)} collective-permute-done((bf16[64,512]{1,0:T(8,128)(2,1)S(1)}, bf16[64,512]{1,0:T(8,128)(2,1)S(1)}, u32[]{:S(2)}, u32[]{:S(2)}) %collective-permute-start) | collective-permute-done | bytes 65568 | tf_op jit(solution)/shard_map/ppermute | solution.py:183
  44.0 1.9 %collective-permute-start.1 = (bf16[128,512]{1,0:T(8,128)(2,1)S(1)}, bf16[128,512]{1,0:T(8,128)(2,1)S(1)}, u32[]{:S(2)}, u32[]{:S(2)}) collective-permute-start(bf16[128,512]{1,0:T(8,128)(2,1)S(1)} %pad_maximum_fusion), channel_id=1, source_target_pairs={{0,2},{1,3},{2,0},{3,1},{4,6},{5,7},{6,4},{7,5},{8,10},{9,11},{10,... | collective-permute-start | bytes 393224 | tf_op jit(solution)/shard_map/ppermute | solution.py:183
  45.9 4.0 %all-to-all-done.1 = bf16[64,13,2,128]{3,2,1,0:T(2,128)(2,1)S(1)} async-done(((bf16[64,13,2,128]{3,2,1,0:T(2,128)(2,1)}), bf16[64,13,2,128]{3,2,1,0:T(2,128)(2,1)S(1)}, u32[]{:S(2)}, u32[]{:S(2)}) %all-to-all-start.1) | async-done | bytes 426016 | tf_op jit(solution)/shard_map/all_to_all | solution.py:225
  49.9 1.3 %shard_map.169 = (f32[512,128]{1,0:T(8,128)}, f32[8,128]{1,0:T(8,128)S(1)}) custom-call(bf16[1664,128]{1,0:T(8,128)(2,1)S(1)} %bitcast.14), custom_call_target="tpu_custom_call" | custom-call | tf_op jit(solution)/shard_map/pallas_call | solution.py:166
  51.3 0.0 copy-start.2
  51.3 12.6 %all-to-all-start.2 = ((f32[512,1,128]{2,1,0:T(1,128)}), f32[512,1,128]{2,1,0:T(1,128)S(1)}, u32[]{:S(2)}, u32[]{:S(2)}) async-start(f32[512,1,128]{2,1,0:T(1,128)} %bitcast.10), calls=%async_computation.2 | async-start | bytes 524288 | tf_op jit(solution)/shard_map/all_to_all | solution.py:235
  63.9 0.0 copy-start.1
  63.9 0.0 collective-permute-done.1
  64.0 3.4 %collective-permute-start.2 = (bf16[256,512]{1,0:T(8,128)(2,1)S(1)}, bf16[256,512]{1,0:T(8,128)(2,1)S(1)}, u32[]{:S(2)}, u32[]{:S(2)}) collective-permute-start(bf16[256,512]{1,0:T(8,128)(2,1)S(1)} %constant_dynamic-update-slice_fusion.up_ref), channel_id=1, source_target_pairs={{0,1},{1,0},{2,3},{3,2},{4,5},{5,4},{6,7},{7,6},{8,9},{9,8},{10,11... | collective-permute-start | bytes 786440 | tf_op jit(solution)/shard_map/ppermute | solution.py:183
  67.4 13.9 %all-to-all-done.2 = f32[512,1,128]{2,1,0:T(1,128)S(1)} async-done(((f32[512,1,128]{2,1,0:T(1,128)}), f32[512,1,128]{2,1,0:T(1,128)S(1)}, u32[]{:S(2)}, u32[]{:S(2)}) %all-to-all-start.2) | async-done | bytes 262176 | tf_op jit(solution)/shard_map/all_to_all | solution.py:235
  81.3 0.0 collective-permute-done.2.other_ref
  81.3 0.0 copy-done.2
  81.3 0.0 copy-done.1
  81.3 0.0 copy-start.3
  81.3 0.0 copy-start.4
  81.3 1.4 %shard_map.170 = (bf16[128,512]{1,0:T(8,128)(2,1)}, bf16[64,8,128]{2,1,0:T(8,128)(2,1)S(1)}) custom-call(bf16[512,128]{1,0:T(8,128)(2,1)S(1)} %bitcast.16, bf16[256,512]{1,0:T(8,128)(2,1)S(1)} %constant_dynamic-update-slice_fusion.up_ref, bf16[256,512]{1,0:T(8,128)(2,1)S(1)} %collective-permute-done.2.other_ref, ...), custom_call_target="tpu_custom_call" | custom-call | tf_op jit(solution)/shard_map/pallas_call | solution.py:166
  82.7 0.0 copy-start.5
  82.7 15.7 %all_to_all.21.arrived_ref = bf16[64,8,128]{2,1,0:T(8,128)(2,1)S(1)} all-to-all(bf16[64,8,128]{2,1,0:T(8,128)(2,1)S(1)} %get-tuple-element.28), channel_id=1, replica_groups=mesh['x'=4,'z'=8,'core'=2,'basis'=8] {'x','z','core'}, dimensions={0} | all-to-all | bytes 262144 | tf_op jit(solution)/shard_map/all_to_all | solution.py:247
  98.4 0.0 copy-done.3
  98.4 0.0 copy-done.4
  98.4 0.0 copy-done.5
  98.4 1.1 %shard_map.171 = bf16[32,512]{1,0:T(8,128)(2,1)} custom-call(bf16[64,8,128]{2,1,0:T(8,128)(2,1)S(1)} %all_to_all.21.arrived_ref, f32[8,128]{1,0:T(8,128)S(1)} %get-tuple-element.29.ids_ref, bf16[32,512]{1,0:T(8,128)(2,1)S(1)} %copy-done.5, bf16[512,512]{1,0:T(8,128)(2,1)S(1)} %copy-done.3, bf16[512,512]{1,0:T(8,128)(2,1)S(1)} %copy-done.4), custom_call_target="tpu_custom_call" | custom-call | tf_op jit(solution)/shard_map/pallas_call | solution.py:166
  (5 shorter events, 0.0 us)
Async XLA Ops:
  0.6 17.0 %copy-start = (bf16[24,1,128,128]{3,2,1,0:T(8,128)(2,1)S(1)}, bf16[24,1,128,128]{3,2,1,0:T(8,128)(2,1)}, u32[]{:S(2)}) copy-start(bf16[24,1,128,128]{3,2,1,0:T(8,128)(2,1)} %param.19) | copy-start | bytes 2359300
  19.1 15.6 %copy-start.6 = (bf16[1,64,512]{2,1,0:T(8,128)(2,1)S(1)}, bf16[1,64,512]{2,1,0:T(8,128)(2,1)}, u32[]{:S(2)}) copy-start(bf16[1,64,512]{2,1,0:T(8,128)(2,1)} %param.23) | copy-start | bytes 196612
  19.1 30.9 %all-to-all-start.1 = ((bf16[64,13,2,128]{3,2,1,0:T(2,128)(2,1)}), bf16[64,13,2,128]{3,2,1,0:T(2,128)(2,1)S(1)}, u32[]{:S(2)}, u32[]{:S(2)}) async-start(bf16[64,13,2,128]{3,2,1,0:T(2,128)(2,1)} %bitcast.7), calls=%async_computation.1 | async-start | bytes 851968 | tf_op jit(solution)/shard_map/all_to_all | solution.py:225
  34.7 9.3 %collective-permute-start = (bf16[64,512]{1,0:T(8,128)(2,1)S(1)}, bf16[64,512]{1,0:T(8,128)(2,1)S(1)}, u32[]{:S(2)}, u32[]{:S(2)}) collective-permute-start(bf16[64,512]{1,0:T(8,128)(2,1)S(1)} %bitcast.18), channel_id=1, source_target_pairs={{0,4},{1,5},{2,6},{3,7},{4,0},{5,1},{6,2},{7,3},{8,12},{9,13},{10,... | collective-permute-start | bytes 196616 | tf_op jit(solution)/shard_map/ppermute | solution.py:183
  44.0 19.9 %collective-permute-start.1 = (bf16[128,512]{1,0:T(8,128)(2,1)S(1)}, bf16[128,512]{1,0:T(8,128)(2,1)S(1)}, u32[]{:S(2)}, u32[]{:S(2)}) collective-permute-start(bf16[128,512]{1,0:T(8,128)(2,1)S(1)} %pad_maximum_fusion), channel_id=1, source_target_pairs={{0,2},{1,3},{2,0},{3,1},{4,6},{5,7},{6,4},{7,5},{8,10},{9,11},{10,... | collective-permute-start | bytes 393224 | tf_op jit(solution)/shard_map/ppermute | solution.py:183
  51.3 30.0 %copy-start.2 = (bf16[512,512]{1,0:T(8,128)(2,1)S(1)}, bf16[512,512]{1,0:T(8,128)(2,1)}, u32[]{:S(2)}) copy-start(bf16[512,512]{1,0:T(8,128)(2,1)} %second_ref.2) | copy-start | bytes 1572868
  51.3 30.0 %all-to-all-start.2 = ((f32[512,1,128]{2,1,0:T(1,128)}), f32[512,1,128]{2,1,0:T(1,128)S(1)}, u32[]{:S(2)}, u32[]{:S(2)}) async-start(f32[512,1,128]{2,1,0:T(1,128)} %bitcast.10), calls=%async_computation.2 | async-start | bytes 524288 | tf_op jit(solution)/shard_map/all_to_all | solution.py:235
  63.9 17.4 %copy-start.1 = (bf16[512,512]{1,0:T(8,128)(2,1)S(1)}, bf16[512,512]{1,0:T(8,128)(2,1)}, u32[]{:S(2)}) copy-start(bf16[512,512]{1,0:T(8,128)(2,1)} %first_ref.2) | copy-start | bytes 1572868
  64.0 17.3 %collective-permute-start.2 = (bf16[256,512]{1,0:T(8,128)(2,1)S(1)}, bf16[256,512]{1,0:T(8,128)(2,1)S(1)}, u32[]{:S(2)}, u32[]{:S(2)}) collective-permute-start(bf16[256,512]{1,0:T(8,128)(2,1)S(1)} %constant_dynamic-update-slice_fusion.up_ref), channel_id=1, source_target_pairs={{0,1},{1,0},{2,3},{3,2},{4,5},{5,4},{6,7},{7,6},{8,9},{9,8},{10,11... | collective-permute-start | bytes 786440 | tf_op jit(solution)/shard_map/ppermute | solution.py:183
  81.3 17.1 %copy-start.3 = (bf16[512,512]{1,0:T(8,128)(2,1)S(1)}, bf16[512,512]{1,0:T(8,128)(2,1)}, u32[]{:S(2)}) copy-start(bf16[512,512]{1,0:T(8,128)(2,1)} %first_ref.3) | copy-start | bytes 1572868
  81.3 17.1 %copy-start.4 = (bf16[512,512]{1,0:T(8,128)(2,1)S(1)}, bf16[512,512]{1,0:T(8,128)(2,1)}, u32[]{:S(2)}) copy-start(bf16[512,512]{1,0:T(8,128)(2,1)} %second_ref.3) | copy-start | bytes 1572868
  82.7 15.7 %copy-start.5 = (bf16[32,512]{1,0:T(8,128)(2,1)S(1)}, bf16[32,512]{1,0:T(8,128)(2,1)}, u32[]{:S(2)}) copy-start(bf16[32,512]{1,0:T(8,128)(2,1)} %feats_ref.1) | copy-start | bytes 98308

commit v6 on v5

--- a/solution.py
+++ b/solution.py
@@ -9,9 +9,11 @@
 f32, bf16, i32 = jnp.float32, jnp.bfloat16, jnp.int32
 VMEM = pl.BlockSpec(memory_space=pltpu.VMEM)
 SMEM = pl.BlockSpec(memory_space=pltpu.SMEM)
+ANY = pl.BlockSpec(memory_space=pl.ANY)
 GRAPH = ("x", "z", "core")
 STEPS = (4, 2, 1)
 ORDER = (0, 4, 2, 6)
+SAVES = 4
 HEAD = 8
 OFFSET = 256
 
@@ -140,7 +142,15 @@
     send_ref[...] = scratch[...].reshape(send_ref.shape).astype(bf16)
 
 
-def atom_kernel(arrived_ref, ids_ref, feats_ref, first_ref, second_ref, out_ref, scratch):
+def atom_kernel(
+    arrived_ref, ids_ref, feats_ref, first_ref, second_ref, update_ref, out_ref, saved_ref, scratch, sem
+):
+    step = update_ref.shape[0] // SAVES
+    saves = []
+    for i in range(SAVES):
+        span = pl.ds(i * step, step)
+        saves.append(pltpu.make_async_copy(update_ref.at[span], saved_ref.at[span], sem.at[i]))
+        saves[-1].start()
     places = arrived_ref.shape[0] * 2
     count, width = feats_ref.shape
     chunks = width // 128
@@ -156,9 +166,11 @@
     ).astype(bf16)
     hidden = silu(dot(gathered, first_ref[...], 1, 0)).astype(bf16)
     out_ref[...] = (feats_ref[...].astype(f32) + dot(hidden, second_ref[...], 1, 0)).astype(bf16)
-
-
-def call(kernel, specs, outs, *args, scratch=(), keep=(), scalar=(), space=pltpu.VMEM):
+    for save in saves:
+        save.wait()
+
+
+def call(kernel, specs, outs, *args, scratch=(), keep=(), hand=(), scalar=(), space=pltpu.VMEM):
     args = [
         pltpu.with_memory_space_constraint(a, space) if s is VMEM or space is pltpu.HBM else a
         for a, s in zip(args, specs)
@@ -166,10 +178,10 @@
     return pl.pallas_call(
         kernel,
         in_specs=specs,
-        out_specs=[SMEM if i in scalar else VMEM for i in range(len(outs))],
+        out_specs=[SMEM if i in scalar else ANY if i in hand else VMEM for i in range(len(outs))],
         out_shape=[
             jax.ShapeDtypeStruct(shape, dtype)
-            if i in keep
+            if i in keep + hand
             else (pltpu.SMEM if i in scalar else pltpu.VMEM)(shape, dtype)
             for i, (shape, dtype) in enumerate(outs)
         ],
@@ -241,14 +253,14 @@
         edge_kernel, [VMEM] * 7,
         [((rows, width), bf16), ((peers, 2 * width // 128, 128), bf16)],
         columns.reshape(peers * blocks, 128), ups, other, edges,
-        res_first, res_second, head, keep=(0,),
+        res_first, res_second, head,
         scratch=[pltpu.VMEM((peers * 2 * width // 128, 128), f32)],
     )
     arrived = lax.all_to_all(send, GRAPH, 0, 0, tiled=True)
-    (atom_update,) = call(
-        atom_kernel, [VMEM] * 5, [(atom_feats.shape, bf16)],
-        arrived, ids, atom_feats, atom_first, atom_second, keep=(0,),
-        scratch=[pltpu.VMEM((peers * 2 * width // 128, 128), f32)],
+    atom_update, edge_update = call(
+        atom_kernel, [VMEM] * 6, [(atom_feats.shape, bf16), (edge_update.shape, bf16)],
+        arrived, ids, atom_feats, atom_first, atom_second, edge_update, keep=(0,), hand=(1,),
+        scratch=[pltpu.VMEM((peers * 2 * width // 128, 128), f32), pltpu.SemaphoreType.DMA((SAVES,))],
     )
     return (edge_update, atom_update)
 

time: 100 us -> 99.6 us (level)
  no operation moved by 1% of the time
where the time goes in v6:
time: 99.6 us; the launch traced here: 99.2 us
  starting transfers between devices  35.6 us (36%)
  blocking collectives  30.9 us (31%)
  waiting for transfers between devices  25 us (25%)
  Pallas kernels  6.67 us (7%)
    all_to_all x1, starting transfers between devices, body(): lax.all_to_all(send.reshape(peers, packed // 2, 2, 128), GRAPH, 0, 0, til...  15.6 us
    all_to_all x1, blocking collectives, body(): arrived = lax.all_to_all(send, GRAPH, 0, 0, tiled=True)  15.6 us
    all_to_all x1, blocking collectives, body(): lowered = lax.all_to_all(lowered, 'basis', 0, 0, tiled=True)  15.4 us
    all_to_all x1, waiting for transfers between devices, body(): lax.all_to_all(summed.reshape(peers * blocks, 1, 128), ('basis',) + GRAPH...  13.9 us
    all_to_all x1, starting transfers between devices, body(): lax.all_to_all(summed.reshape(peers * blocks, 1, 128), ('basis',) + GRAPH...  12.6 us
    ppermute x3, starting transfers between devices, shifted(): return lax.ppermute(x, 'basis', order)  7.48 us
    ppermute x3, waiting for transfers between devices, shifted(): return lax.ppermute(x, 'basis', order)  7.14 us
    pallas_call x5, Pallas kernels, call(): pl.pallas_call(kernel, in_specs=specs, out_specs=[SMEM if i in scalar els...  6.67 us
  transfers between devices with their start and end apart: 5, of which 3 were waited for; matrix products, arithmetic and copies ran while one was open for 0% of the time, Pallas kernels for 1%

profile of v6, /device:TPU:1, one launch (start us, length us, event | category | flops | bytes accessed | tf_op | source)
XLA Modules:
  0.0 99.2 jit_solution(13873874765642833583)
XLA Ops:
  0.6 0.0 copy-start
  0.6 1.6 %shard_map.167 = (bf16[8,64,128]{2,1,0:T(8,128)(2,1)S(1)}, f32[8,128]{1,0:T(8,128)S(1)}, f32[64,128]{1,0:T(8,128)S(1)}, s32[1,24]{1,0:T(1,128)S(4)}, bf16[128,512]{1,0:T(8,128)(2,1)S(1)}) custom-call(bf16[128,512]{1,0:T(8,128)(2,1)} %refs_0_.1, bf16[512,512]{1,0:T(8,128)(2,1)} %refs_1_.1, bf16[64,512]{1,0:T(8,128)(2,1)} %bitcast.21, s32[1,24]{1,0:T(1,128)} %bitcast.22, ...), custom_call_target="tpu_custom_call" | custom-call | tf_op jit(solution)/shard_map/pallas_call | solution.py:178
  2.3 15.4 %all_to_all.20.lowered_ref = bf16[8,64,128]{2,1,0:T(8,128)(2,1)S(1)} all-to-all(bf16[8,64,128]{2,1,0:T(8,128)(2,1)S(1)} %get-tuple-element.20), channel_id=1, replica_groups=mesh['x'=4,'z'=8,'core'=2,'basis'=8] {'basis'}, dimensions={0} | all-to-all | bytes 262144 | tf_op jit(solution)/shard_map/all_to_all | solution.py:230
  17.6 0.0 copy-done
  17.7 1.4 %shard_map.168 = bf16[1664,128]{1,0:T(8,128)(2,1)} custom-call(s32[1,24]{1,0:T(1,128)S(4)} %get-tuple-element.18.source_ref, bf16[8,64,128]{2,1,0:T(8,128)(2,1)S(1)} %all_to_all.20.lowered_ref, bf16[24,128,128]{2,1,0:T(8,128)(2,1)S(1)} %bitcast.15, f32[8,128]{1,0:T(8,128)S(1)} %get-tuple-element.22.head_ref, f32[64,128]{1,0:T(8,128)S(1)} %get-tuple-element.23.atoms_ref), custom_call_target="tpu_custom_call" | custom-call | tf_op jit(solution)/shard_map/pallas_call | solution.py:178
  19.1 0.0 copy-start.6
  19.1 15.6 %all-to-all-start.1 = ((bf16[64,13,2,128]{3,2,1,0:T(2,128)(2,1)}), bf16[64,13,2,128]{3,2,1,0:T(2,128)(2,1)S(1)}, u32[]{:S(2)}, u32[]{:S(2)}) async-start(bf16[64,13,2,128]{3,2,1,0:T(2,128)(2,1)} %bitcast.7), calls=%async_computation.1 | async-start | bytes 851968 | tf_op jit(solution)/shard_map/all_to_all | solution.py:237
  34.7 0.0 copy-done.6
  34.7 2.2 %collective-permute-start = (bf16[64,512]{1,0:T(8,128)(2,1)S(1)}, bf16[64,512]{1,0:T(8,128)(2,1)S(1)}, u32[]{:S(2)}, u32[]{:S(2)}) collective-permute-start(bf16[64,512]{1,0:T(8,128)(2,1)S(1)} %bitcast.18), channel_id=1, source_target_pairs={{0,4},{1,5},{2,6},{3,7},{4,0},{5,1},{6,2},{7,3},{8,12},{9,13},{10,... | collective-permute-start | bytes 196616 | tf_op jit(solution)/shard_map/ppermute | solution.py:195
  36.9 7.1 %collective-permute-done = bf16[64,512]{1,0:T(8,128)(2,1)S(1)} collective-permute-done((bf16[64,512]{1,0:T(8,128)(2,1)S(1)}, bf16[64,512]{1,0:T(8,128)(2,1)S(1)}, u32[]{:S(2)}, u32[]{:S(2)}) %collective-permute-start) | collective-permute-done | bytes 65568 | tf_op jit(solution)/shard_map/ppermute | solution.py:195
  44.0 1.9 %collective-permute-start.1 = (bf16[128,512]{1,0:T(8,128)(2,1)S(1)}, bf16[128,512]{1,0:T(8,128)(2,1)S(1)}, u32[]{:S(2)}, u32[]{:S(2)}) collective-permute-start(bf16[128,512]{1,0:T(8,128)(2,1)S(1)} %pad_maximum_fusion), channel_id=1, source_target_pairs={{0,2},{1,3},{2,0},{3,1},{4,6},{5,7},{6,4},{7,5},{8,10},{9,11},{10,... | collective-permute-start | bytes 393224 | tf_op jit(solution)/shard_map/ppermute | solution.py:195
  45.9 4.0 %all-to-all-done.1 = bf16[64,13,2,128]{3,2,1,0:T(2,128)(2,1)S(1)} async-done(((bf16[64,13,2,128]{3,2,1,0:T(2,128)(2,1)}), bf16[64,13,2,128]{3,2,1,0:T(2,128)(2,1)S(1)}, u32[]{:S(2)}, u32[]{:S(2)}) %all-to-all-start.1) | async-done | bytes 426016 | tf_op jit(solution)/shard_map/all_to_all | solution.py:237
  49.9 1.3 %shard_map.169 = (f32[512,128]{1,0:T(8,128)}, f32[8,128]{1,0:T(8,128)S(1)}) custom-call(bf16[1664,128]{1,0:T(8,128)(2,1)S(1)} %bitcast.14), custom_call_target="tpu_custom_call" | custom-call | tf_op jit(solution)/shard_map/pallas_call | solution.py:178
  51.3 0.0 copy-start.2
  51.3 12.6 %all-to-all-start.2 = ((f32[512,1,128]{2,1,0:T(1,128)}), f32[512,1,128]{2,1,0:T(1,128)S(1)}, u32[]{:S(2)}, u32[]{:S(2)}) async-start(f32[512,1,128]{2,1,0:T(1,128)} %bitcast.10), calls=%async_computation.2 | async-start | bytes 524288 | tf_op jit(solution)/shard_map/all_to_all | solution.py:247
  63.9 0.0 copy-start.1
  63.9 0.0 collective-permute-done.1
  63.9 3.4 %collective-permute-start.2 = (bf16[256,512]{1,0:T(8,128)(2,1)S(1)}, bf16[256,512]{1,0:T(8,128)(2,1)S(1)}, u32[]{:S(2)}, u32[]{:S(2)}) collective-permute-start(bf16[256,512]{1,0:T(8,128)(2,1)S(1)} %constant_dynamic-update-slice_fusion.up_ref), channel_id=1, source_target_pairs={{0,1},{1,0},{2,3},{3,2},{4,5},{5,4},{6,7},{7,6},{8,9},{9,8},{10,11... | collective-permute-start | bytes 786440 | tf_op jit(solution)/shard_map/ppermute | solution.py:195
  67.3 13.9 %all-to-all-done.2 = f32[512,1,128]{2,1,0:T(1,128)S(1)} async-done(((f32[512,1,128]{2,1,0:T(1,128)}), f32[512,1,128]{2,1,0:T(1,128)S(1)}, u32[]{:S(2)}, u32[]{:S(2)}) %all-to-all-start.2) | async-done | bytes 262176 | tf_op jit(solution)/shard_map/all_to_all | solution.py:247
  81.2 0.0 collective-permute-done.2.other_ref
  81.2 0.0 copy-done.2
  81.3 0.0 copy-done.1
  81.3 0.0 copy-start.3
  81.3 0.0 copy-start.4
  81.3 0.9 shard_map.170
  82.2 0.0 copy-start.5
  82.2 15.6 %all_to_all.21.arrived_ref = bf16[64,8,128]{2,1,0:T(8,128)(2,1)S(1)} all-to-all(bf16[64,8,128]{2,1,0:T(8,128)(2,1)S(1)} %get-tuple-element.29), channel_id=1, replica_groups=mesh['x'=4,'z'=8,'core'=2,'basis'=8] {'x','z','core'}, dimensions={0} | all-to-all | bytes 262144 | tf_op jit(solution)/shard_map/all_to_all | solution.py:259
  97.8 0.0 copy-done.3
  97.8 0.0 copy-done.4
  97.8 0.0 copy-done.5
  97.8 1.4 %shard_map.171 = (bf16[32,512]{1,0:T(8,128)(2,1)}, bf16[128,512]{1,0:T(8,128)(2,1)}) custom-call(bf16[64,8,128]{2,1,0:T(8,128)(2,1)S(1)} %all_to_all.21.arrived_ref, f32[8,128]{1,0:T(8,128)S(1)} %get-tuple-element.30.ids_ref, bf16[32,512]{1,0:T(8,128)(2,1)S(1)} %copy-done.5, bf16[512,512]{1,0:T(8,128)(2,1)S(1)} %copy-done.3, bf16[512,512]{1,0:T(8,128)(2,1)S(1)} %copy-done.4, ...), custom_call_target="tpu_custom_call" | custom-call | tf_op jit(solution)/shard_map/pallas_call | solution.py:178
  (5 shorter events, 0.0 us)
Async XLA Ops:
  0.6 17.0 %copy-start = (bf16[24,1,128,128]{3,2,1,0:T(8,128)(2,1)S(1)}, bf16[24,1,128,128]{3,2,1,0:T(8,128)(2,1)}, u32[]{:S(2)}) copy-start(bf16[24,1,128,128]{3,2,1,0:T(8,128)(2,1)} %param.19) | copy-start | bytes 2359300
  19.1 15.6 %copy-start.6 = (bf16[1,64,512]{2,1,0:T(8,128)(2,1)S(1)}, bf16[1,64,512]{2,1,0:T(8,128)(2,1)}, u32[]{:S(2)}) copy-start(bf16[1,64,512]{2,1,0:T(8,128)(2,1)} %param.23) | copy-start | bytes 196612
  19.1 30.9 %all-to-all-start.1 = ((bf16[64,13,2,128]{3,2,1,0:T(2,128)(2,1)}), bf16[64,13,2,128]{3,2,1,0:T(2,128)(2,1)S(1)}, u32[]{:S(2)}, u32[]{:S(2)}) async-start(bf16[64,13,2,128]{3,2,1,0:T(2,128)(2,1)} %bitcast.7), calls=%async_computation.1 | async-start | bytes 851968 | tf_op jit(solution)/shard_map/all_to_all | solution.py:237
  34.7 9.3 %collective-permute-start = (bf16[64,512]{1,0:T(8,128)(2,1)S(1)}, bf16[64,512]{1,0:T(8,128)(2,1)S(1)}, u32[]{:S(2)}, u32[]{:S(2)}) collective-permute-start(bf16[64,512]{1,0:T(8,128)(2,1)S(1)} %bitcast.18), channel_id=1, source_target_pairs={{0,4},{1,5},{2,6},{3,7},{4,0},{5,1},{6,2},{7,3},{8,12},{9,13},{10,... | collective-permute-start | bytes 196616 | tf_op jit(solution)/shard_map/ppermute | solution.py:195
  44.0 19.9 %collective-permute-start.1 = (bf16[128,512]{1,0:T(8,128)(2,1)S(1)}, bf16[128,512]{1,0:T(8,128)(2,1)S(1)}, u32[]{:S(2)}, u32[]{:S(2)}) collective-permute-start(bf16[128,512]{1,0:T(8,128)(2,1)S(1)} %pad_maximum_fusion), channel_id=1, source_target_pairs={{0,2},{1,3},{2,0},{3,1},{4,6},{5,7},{6,4},{7,5},{8,10},{9,11},{10,... | collective-permute-start | bytes 393224 | tf_op jit(solution)/shard_map/ppermute | solution.py:195
  51.3 30.0 %copy-start.2 = (bf16[512,512]{1,0:T(8,128)(2,1)S(1)}, bf16[512,512]{1,0:T(8,128)(2,1)}, u32[]{:S(2)}) copy-start(bf16[512,512]{1,0:T(8,128)(2,1)} %second_ref.2) | copy-start | bytes 1572868
  51.3 29.9 %all-to-all-start.2 = ((f32[512,1,128]{2,1,0:T(1,128)}), f32[512,1,128]{2,1,0:T(1,128)S(1)}, u32[]{:S(2)}, u32[]{:S(2)}) async-start(f32[512,1,128]{2,1,0:T(1,128)} %bitcast.10), calls=%async_computation.2 | async-start | bytes 524288 | tf_op jit(solution)/shard_map/all_to_all | solution.py:247
  63.9 17.4 %copy-start.1 = (bf16[512,512]{1,0:T(8,128)(2,1)S(1)}, bf16[512,512]{1,0:T(8,128)(2,1)}, u32[]{:S(2)}) copy-start(bf16[512,512]{1,0:T(8,128)(2,1)} %first_ref.2) | copy-start | bytes 1572868
  63.9 17.3 %collective-permute-start.2 = (bf16[256,512]{1,0:T(8,128)(2,1)S(1)}, bf16[256,512]{1,0:T(8,128)(2,1)S(1)}, u32[]{:S(2)}, u32[]{:S(2)}) collective-permute-start(bf16[256,512]{1,0:T(8,128)(2,1)S(1)} %constant_dynamic-update-slice_fusion.up_ref), channel_id=1, source_target_pairs={{0,1},{1,0},{2,3},{3,2},{4,5},{5,4},{6,7},{7,6},{8,9},{9,8},{10,11... | collective-permute-start | bytes 786440 | tf_op jit(solution)/shard_map/ppermute | solution.py:195
  81.3 16.5 %copy-start.3 = (bf16[512,512]{1,0:T(8,128)(2,1)S(1)}, bf16[512,512]{1,0:T(8,128)(2,1)}, u32[]{:S(2)}) copy-start(bf16[512,512]{1,0:T(8,128)(2,1)} %first_ref.3) | copy-start | bytes 1572868
  81.3 16.5 %copy-start.4 = (bf16[512,512]{1,0:T(8,128)(2,1)S(1)}, bf16[512,512]{1,0:T(8,128)(2,1)}, u32[]{:S(2)}) copy-start(bf16[512,512]{1,0:T(8,128)(2,1)} %second_ref.3) | copy-start | bytes 1572868
  82.2 15.6 %copy-start.5 = (bf16[32,512]{1,0:T(8,128)(2,1)S(1)}, bf16[32,512]{1,0:T(8,128)(2,1)}, u32[]{:S(2)}) copy-start(bf16[32,512]{1,0:T(8,128)(2,1)} %feats_ref.1) | copy-start | bytes 98308
